TPU v7x, 512 devices: a whole 4x4x16 slice. The times are simulated.
512 devices in a mesh: ctx: 64 (over z, y), tp: 8 (over x, core).
Axes of the slice: x: 4, y: 4, z: 16, core: 2. Of those that a mesh axis runs over, the one named last changes fastest.
Arguments:
- queries: bfloat16 [8192, 2048], P('ctx', 'tp'), may hold values from -6 to 6
- key_vectors: bfloat16 [8192, 2, 2048], P('ctx', None, 'tp'), may hold values from -40 to 40
- value_vectors: bfloat16 [8192, 2, 2048], P('ctx', None, 'tp'), may hold values from -40 to 40
- strengths: float32 [2, 16, 8192], P(None, 'tp', 'ctx'), may hold values from 0 to 2
- log_gate: float32 [16, 8192], P('tp', 'ctx'), may hold values from -2 to 0
- out_gain: float32 [2048], P('tp'), may hold values from 0.1 to 1.9
- out_weight: bfloat16 [2048, 4096], P('tp'), may hold values from -0.125 to 0.125
Outputs:
- layer_out: bfloat16 [8192, 4096], P('ctx', 'tp')
All inputs are finite; a program needn't handle non-finite values.
Results may differ from a plain program's by a relative error of at most 0.019.
Values may be sent and summed in bfloat16 or wider, within the bound.
A program may use at most 64 MiB of HBM per device.

v0:
```python
import jax
import jax.numpy as jnp
from jax import lax
from jax.sharding import PartitionSpec as P

highest = lax.Precision.HIGHEST


def carried_in(x, axis, combine, identity):
    devices, position = (lax.axis_size(axis), lax.axis_index(axis))
    everything = jax.tree.map(lambda part: lax.all_gather(part, axis), x)
    start = jax.tree.map(
        lambda part, zero: jnp.broadcast_to(jnp.asarray(zero, part.dtype), part.shape), x, identity
    )

    def step(k, before):
        reached = k < position
        new = combine(before, jax.tree.map(lambda part: part[k], everything))
        return jax.tree.map(lambda a, b: jnp.where(reached, a, b), new, before)

    return lax.fori_loop(0, devices, step, start)


def matmul_heads(left_side, right_side):
    return jnp.einsum("...ij,...jk->...ik", left_side, right_side, precision=highest)


def combine_pairs(earlier, latter):
    return (matmul_heads(latter[0], earlier[0]), matmul_heads(latter[0], earlier[1]) + latter[1])


def solve_lower(system, right_side):
    return jax.scipy.linalg.solve_triangular(system, right_side, lower=True, unit_diagonal=True)


def local(queries, key_vectors, value_vectors, strengths, log_gate, out_gain, out_weight):
    tokens = queries.shape[0]
    head_count = log_gate.shape[0]
    key_width = key_vectors.shape[2] // head_count
    value_width = value_vectors.shape[2] // head_count
    block_span = min(64, tokens // 2)
    block_list = tokens // block_span
    step_count = 2 * block_span
    key_rows = key_vectors.astype(jnp.float32).reshape(tokens, 2, head_count, key_width)
    key_rows = key_rows / jnp.sqrt(jnp.sum(key_rows * key_rows, axis=-1, keepdims=True) + 1e-06)
    key_rows = key_rows.reshape(block_list, block_span, 2, head_count, key_width).transpose(
        0, 3, 1, 2, 4
    )
    key_rows = key_rows.reshape(block_list, head_count, step_count, key_width)
    value_rows = value_vectors.astype(jnp.float32).reshape(
        block_list, block_span, 2, head_count, value_width
    )
    value_rows = value_rows.transpose(0, 3, 1, 2, 4).reshape(
        block_list, head_count, step_count, value_width
    )
    query_rows = (
        queries.astype(jnp.float32)
        .reshape(block_list, block_span, head_count, key_width)
        .transpose(0, 2, 1, 3)
    )
    strength_rows = strengths.reshape(2, head_count, block_list, block_span).transpose(2, 1, 3, 0)
    strength_rows = strength_rows.reshape(block_list, head_count, step_count)
    gate_rows = log_gate.reshape(head_count, block_list, block_span).transpose(1, 0, 2)
    decay_rows = jnp.stack([gate_rows, jnp.zeros_like(gate_rows)], axis=-1).reshape(
        block_list, head_count, step_count
    )
    cumulative = jnp.cumsum(decay_rows, axis=-1)
    later_index = lax.broadcasted_iota(jnp.int32, (step_count, step_count), 0)
    earlier_index = lax.broadcasted_iota(jnp.int32, (step_count, step_count), 1)
    inclusive = later_index >= earlier_index
    strict = later_index > earlier_index
    spread = cumulative[..., :, None] - cumulative[..., None, :]
    ratios = jnp.where(inclusive, jnp.exp(jnp.where(inclusive, spread, 0.0)), 0.0)
    intersection = jnp.einsum("bhid,bhmd->bhim", key_rows, key_rows, precision=highest)
    system = jnp.eye(step_count, dtype=jnp.float32) + jnp.where(
        strict, strength_rows[..., :, None] * ratios * intersection, 0.0
    )
    right_side = jnp.concatenate(
        [
            strength_rows[..., None] * value_rows,
            (strength_rows * jnp.exp(cumulative))[..., None] * key_rows,
        ],
        axis=-1,
    )
    solved_system = jax.vmap(solve_lower)(
        system.reshape(block_list * head_count, step_count, step_count),
        right_side.reshape(block_list * head_count, step_count, value_width + key_width),
    )
    solved_system = solved_system.reshape(
        block_list, head_count, step_count, value_width + key_width
    )
    value_write = solved_system[..., :value_width]
    key_write = solved_system[..., value_width:]
    block_decay = cumulative[..., -1]
    tail_decay = jnp.exp(block_decay[..., None] - cumulative)
    key_identity = jnp.eye(key_width, dtype=jnp.float32)
    tail_keys = key_rows * tail_decay[..., None]
    transition = jnp.exp(block_decay)[..., None, None] * key_identity - jnp.einsum(
        "bhmd,bhme->bhde", tail_keys, key_write, precision=highest
    )
    offset = jnp.einsum("bhmd,bhme->bhde", tail_keys, value_write, precision=highest)
    query_weights = ratios[..., 1::2, :] * jnp.einsum(
        "bhtd,bhmd->bhtm", query_rows, key_rows, precision=highest
    )
    query_decay = jnp.exp(cumulative[..., 1::2])
    start_moves = jnp.broadcast_to(key_identity, (head_count, key_width, key_width))
    start_state = jnp.zeros((head_count, key_width, value_width), jnp.float32)

    def compose(state_pair, block_pair):
        return (combine_pairs(state_pair, block_pair), state_pair)

    shard_pair, block_starts = lax.scan(compose, (start_moves, start_state), (transition, offset))
    prefix_moves, entering_memory = carried_in(
        (shard_pair[0], shard_pair[1]), "ctx", combine_pairs, (start_moves, start_state)
    )

    def advance(state_now, block_items):
        query_block, weight_block, decay_block, value_block, key_block, move_block, offset_block = (
            block_items
        )
        pseudo = value_block - matmul_heads(key_block, state_now)
        out_rows = decay_block[..., None] * matmul_heads(query_block, state_now) + matmul_heads(
            weight_block, pseudo
        )
        return (matmul_heads(move_block, state_now) + offset_block, out_rows)

    _, outputs = lax.scan(
        advance,
        entering_memory,
        (query_rows, query_weights, query_decay, value_write, key_write, transition, offset),
    )
    gains = out_gain.reshape(head_count, value_width)
    scale_rows = jnp.sqrt(jnp.mean(outputs * outputs, axis=-1, keepdims=True) + 1e-06)
    normed = (outputs / scale_rows * gains[:, None, :]).astype(jnp.bfloat16)
    normed = normed.transpose(0, 2, 1, 3).reshape(tokens, head_count * value_width)
    terms = jnp.dot(normed, out_weight, preferred_element_type=jnp.float32)
    layer_out = lax.psum_scatter(terms.astype(jnp.bfloat16), "tp", scatter_dimension=1, tiled=True)
    return layer_out


def solution(mesh):
    placed = (
        P("ctx", "tp"),
        P("ctx", None, "tp"),
        P("ctx", None, "tp"),
        P(None, "tp", "ctx"),
        P("tp", "ctx"),
        P("tp"),
        P("tp", None),
    )
    return jax.shard_map(
        local, mesh=mesh, in_specs=placed, out_specs=P("ctx", "tp"), check_vma=False
    )
```

profile of v0, /device:TPU:1, one launch (start us, length us, event | category | flops | bytes accessed | tf_op | source)
XLA Modules:
  0.0 504.1 jit_solution(17970500870186570273)
XLA Ops:
  15.3 39.3 %custom-call.4 = f32[4,1,128,128]{2,3,1,0:T(8,128)S(1)} custom-call(f32[4,1,128,128]{3,2,1,0:T(8,128)S(1)} %select_add_fusion), custom_call_target="InvertDiagBlocksLowerTriangular" | custom-call | tf_op jit(solution)/shard_map/vmap(jit(_solve_triangular))/triangular_solve | solution.py:33
  61.7 151.0 %all-gather.5.cloned.1.call-done = f32[128,128,128]{2,1,0:T(8,128)} async-done(((f32[2,128,128]{2,1,0:T(8,128)}), f32[128,128,128]{2,1,0:T(8,128)}) %all-gather.5.cloned.1.call-update) | async-done | bytes 8388624 | tf_op jit(solution)/shard_map/all_gather | solution.py:11
  212.8 154.0 %all-gather.7.cloned.1.call-done = f32[128,128,128]{2,1,0:T(8,128)} async-done(((f32[2,128,128]{2,1,0:T(8,128)}), f32[128,128,128]{2,1,0:T(8,128)}) %all-gather.7.cloned.1.call-update) | async-done | bytes 8388624 | tf_op jit(solution)/shard_map/all_gather | solution.py:11
  366.8 82.6 %while.41 = (s32[]{:T(128)}, f32[2,128,128]{2,1,0:T(8,128)S(1)}, s32[]{:T(128)}, f32[64,2,128,128]{3,2,1,0:T(8,128)}, f32[64,2,128,128]{3,2,1,0:T(8,128)}, /*index=5*/s32[]{:T(128)}, s32[]{:T(128)}) while((s32[]{:T(128)}, f32[2,128,128]{2,1,0:T(8,128)S(1)}, s32[]{:T(128)}, f32[64,2,128,128]{3,2,1,0:T(8,128)}, ...), condition=%wide.region_5.6_spmd.clone, body=%wide.region_4.5_spmd.clone.sunk | while | flops 50462724 | bytes 920159 | solution.py:21
  369.4 1.2 fusion.97
  374.5 1.2 fusion.97
  378.4 1.2 fusion.97
  379.7 1.2 fusion.97
  384.9 1.2 fusion.97
  390.0 1.2 fusion.97
  395.2 1.2 fusion.97
  400.4 1.2 fusion.97
  405.5 1.2 fusion.97
  410.7 1.2 fusion.97
  415.8 1.2 fusion.97
  421.0 1.2 fusion.97
  426.2 1.2 fusion.97
  431.3 1.2 fusion.97
  436.5 1.2 fusion.97
  441.6 1.2 fusion.97
  446.8 1.2 fusion.97
  449.4 3.4 while.39
  455.0 1.4 convolution_convert_fusion
  456.4 41.1 %reduce-scatter.2.cloned.1.call-done = bf16[128,512]{1,0:T(8,128)(2,1)} async-done(((bf16[128,4096]{1,0:T(8,128)(2,1)}), bf16[128,512]{1,0:T(8,128)(2,1)}) %reduce-scatter.2.cloned.1.call-update) | async-done | bytes 131088 | tf_op jit(solution)/shard_map/reduce_scatter | solution.py:137
  (203 shorter events, 81.1 us)
Async XLA Ops:
  6.5 448.4 %copy-start = (bf16[256,4096]{1,0:T(8,128)(2,1)S(1)}, bf16[256,4096]{1,0:T(8,128)(2,1)}, u32[]{:S(2)}) copy-start(bf16[256,4096]{1,0:T(8,128)(2,1)} %param.19) | copy-start | bytes 6291460
  6.5 206.2 %all-gather.5.cloned.1.call-start = ((), (), s32[]{:S(2)}) async-start(), calls=%async_computation.2 | async-start | bytes 8519680 | tf_op jit(solution)/shard_map/all_gather | solution.py:11
  11.8 48.3 %copy-start.4 = (bf16[128,256]{1,0:T(8,128)(2,1)S(1)}, bf16[128,256]{1,0:T(8,128)(2,1)}, u32[]{:S(2)}) copy-start(bf16[128,256]{1,0:T(8,128)(2,1)} %param.13) | copy-start | bytes 196612
  55.5 0.8 copy-start.3
  58.2 0.7 copy-start.1
  58.3 0.7 copy-start.2
  58.9 307.9 %all-gather.7.cloned.1.call-start = ((), (), s32[]{:S(2)}) async-start(), calls=%async_computation.3 | async-start | bytes 8519680 | tf_op jit(solution)/shard_map/all_gather | solution.py:11
  59.7 437.8 %reduce-scatter.2.cloned.1.call-start = ((), (), s32[]{:S(2)}) async-start(), calls=%async_computation.1 | async-start | bytes 1179648 | tf_op jit(solution)/shard_map/reduce_scatter | solution.py:137
  60.1 393.8 %copy-start.5 = (f32[256]{0:T(256)S(1)}, f32[256]{0:T(256)}, u32[]{:S(2)}) copy-start(f32[256]{0:T(256)} %param.18) | copy-start | bytes 3076
Sparse Core Ops, SparseCore 0:
  59.1 153.6 all-gather.4
  215.7 151.0 all-gather.6
  456.5 40.9 reduce-scatter.1
where the time goes:
time: 506 us; the launch traced here: 504 us
  waiting for transfers between devices  347 us (69%)
  matrix products  88.3 us (17%)
  other arithmetic  44.3 us (9%)
  between operations  13.5 us (3%)
  local copies, waits for them, and re-layouts  8.34 us (2%)
    all_gather x2, waiting for transfers between devices, carried_in(): everything = jax.tree.map(lambda part: lax.all_gather(part, axis), x)  305 us
    dot_general x76, matrix products, matmul_heads(): jnp.einsum('...ij,...jk->...ik', left_side, right_side, precision=highest)  83.8 us
    reduce_scatter x1, waiting for transfers between devices, local(): lax.psum_scatter(terms.astype(jnp.bfloat16), 'tp', scatter_dimension=1, t...  41.1 us
    another operation x4, other arithmetic, solve_lower(): jax.scipy.linalg.solve_triangular(system, right_side, lower=True, unit_di...  39.4 us
  transfers between devices with their start and end apart: 3, of which 3 were waited for; matrix products, arithmetic and copies ran while one was open for 0% of the time, Pallas kernels for 0%

commit v1 on v0

v1 whole, which is shorter than its diff:
```python
import functools

import jax
import jax.numpy as jnp
from jax import lax
from jax.experimental import pallas as pl
from jax.experimental.pallas import tpu as pltpu
from jax.sharding import PartitionSpec as P

MESH = pl.DeviceIdType.MESH
F32 = jnp.float32
BF16 = jnp.bfloat16
W = 128


def mm(a, b):
    return jnp.dot(a, b, preferred_element_type=F32)


def mm_nt(a, b):
    return lax.dot_general(a, b, (((1,), (1,)), ((), ())), preferred_element_type=F32)


def split2(a):
    hi = a.astype(BF16)
    return hi, (a - hi.astype(F32)).astype(BF16)


def split3(a):
    hi = a.astype(BF16)
    rest = a - hi.astype(F32)
    mid = rest.astype(BF16)
    return hi, mid, (rest - mid.astype(F32)).astype(BF16)


def dot_pairs(a, b):
    both = mm(jnp.concatenate([a[0], a[1]], axis=1), jnp.concatenate([b[0], b[0]], axis=0))
    return both + mm(a[0], b[1])


def dot_pair_one(a, b):
    return mm(jnp.concatenate([a[0], a[1]], axis=1), jnp.concatenate([b, b], axis=0))


def x3(a, b):
    return dot_pairs(split2(a), split2(b))


def spread_nt(mask, rows):
    hi, mid, lo = split3(rows)
    return mm_nt(mask, hi) + mm_nt(mask, mid) + mm_nt(mask, lo)


def spread_rows(rows, mask):
    hi, mid, lo = split3(rows)
    return mm_nt(hi, mask) + mm_nt(mid, mask) + mm_nt(lo, mask)


def iota(shape, dim):
    return lax.broadcasted_iota(jnp.int32, shape, dim)


def local_maps(keys, values, beta0, beta1, gate):
    heads = len(keys)
    step = iota((2 * W, W), 0)
    token = iota((2 * W, W), 1)
    upto = (2 * token <= step).astype(F32).astype(BF16)
    first = (2 * token == step).astype(F32).astype(BF16)
    second = (2 * token + 1 == step).astype(F32).astype(BF16)
    ones = jnp.ones((W, W), BF16)
    row = iota((W, W), 0)
    col = iota((W, W), 1)
    pre = []
    low = []
    for h in range(heads):
        k = keys[h]
        k32 = k.astype(F32)
        square = split2(k32 * k32)
        inv_col = lax.rsqrt(mm(square[0], ones) + mm(square[1], ones) + 1e-06)
        inv_row = lax.rsqrt(mm_nt(ones, square[0]) + mm_nt(ones, square[1]) + 1e-06)
        g = jnp.broadcast_to(gate[h], (W, W))
        c_col = spread_nt(upto, g)
        c_row = spread_rows(g, upto)
        beta = spread_nt(first, jnp.broadcast_to(beta0[h], (W, W))) + spread_nt(
            second, jnp.broadcast_to(beta1[h], (W, W))
        )
        gram = mm_nt(k, k)
        scaled = beta * inv_col
        blocks = {}
        for a, b in ((0, 0), (1, 1), (1, 0)):
            ra, cb = slice(a * W, a * W + W), slice(b * W, b * W + W)
            diff = c_col[ra] - c_row[:, cb]
            if a == b:
                diff = jnp.where(row > col, diff, -1e30)
            blocks[a, b] = scaled[ra] * jnp.exp(diff) * inv_row[:, cb] * gram[ra, cb]
        grow = jnp.exp(c_col)
        right = jnp.concatenate(
            [scaled * grow * k32, beta * values[h].astype(F32)], axis=1
        )
        last = c_col[2 * W - 1 : 2 * W]
        tail = inv_col * jnp.exp(last - c_col)
        pre.append((blocks[1, 0], right, tail, jnp.exp(last), c_row, inv_row, g))
        low += [blocks[0, 0], blocks[1, 1]]
    eye = (row == col).astype(F32)
    inverse = [
        eye - jnp.where((row == col + 1) & (row % 2 == 1), part, 0.0) for part in low
    ]
    size = 2
    while size < W:
        mask = (row // size == col // size + 1) & ((row // size) % 2 == 1)
        pairs = [split2(t) for t in inverse]
        inner = [
            dot_pairs(split2(jnp.where(mask, part, 0.0)), pair) for part, pair in zip(low, pairs)
        ]
        inverse = [
            t - dot_pairs(pair, split2(c)) for t, pair, c in zip(inverse, pairs, inner)
        ]
        size *= 2
    out = []
    for h in range(heads):
        below, right, tail, decay, c_row, inv_row, g = pre[h]
        top = x3(inverse[2 * h], right[:W])
        bottom = x3(inverse[2 * h + 1], right[W:] - x3(below, top))
        write = jnp.concatenate([top, bottom], axis=0)
        turned = keys[h].astype(F32).T.astype(BF16)
        weighted = split2(jnp.concatenate([tail, tail], axis=1) * write)
        both = mm(turned, weighted[0]) + mm(turned, weighted[1])
        move = jnp.where(row == col, decay, 0.0) - both[:, :W]
        out.append((move, both[:, W:], write, c_row, inv_row, g))
    return out


def local_reads(query, key, made):
    _, _, write, c_row, inv_row, g = made
    row = iota((W, W), 0)
    col = iota((W, W), 1)
    upto = (col <= row).astype(F32).astype(BF16)
    c_tok = spread_nt(upto, g)
    t = iota((W, 2 * W), 0)
    m = iota((W, 2 * W), 1)
    diff = jnp.concatenate([c_tok, c_tok], axis=1) - c_row
    ratio = jnp.exp(jnp.where(m <= 2 * t + 1, diff, -1e30))
    weights = ratio * inv_row * mm_nt(query, key)
    both = x3(weights, write)
    return jnp.exp(c_tok) * query.astype(F32) - both[:, :W], both[:, W:]


def compose(later, earlier):
    move = dot_pairs(later[0], earlier[0])
    offset = dot_pairs(later[0], split2(earlier[1])) + later[1]
    return split2(move), offset


def kernel(
    n_y,
    n_tp,
    q_ref,
    k_ref,
    v_ref,
    beta_ref,
    gate_ref,
    gain_ref,
    w_ref,
    o_ref,
    w_buf,
    y_send,
    y_recv,
    l_send,
    l_recv,
    h_send,
    h_recv,
    pre_m,
    pre_n,
    state,
    s_send,
    s_recv,
    q_eff,
    o_loc,
    n_buf,
    w_ssem,
    w_rsem,
    w_lsem,
    y_ssem,
    y_rsem,
    l_ssem,
    l_rsem,
    h_ssem,
    h_rsem,
    s_ssem,
    s_rsem,
    n_ssem,
    n_rsem,
):
    ctx = lax.axis_index("ctx")
    tp = lax.axis_index("tp")
    y = lax.rem(ctx, n_y)
    z = ctx // n_y
    zl = lax.rem(z, 4)
    zg = z // 4
    core = lax.rem(tp, 2)
    wide = 512

    def at(zz, yy):
        return zz * n_y + yy

    barrier = pltpu.get_barrier_semaphore()
    peers = [(ctx, lax.rem(tp + d, n_tp)) for d in range(1, n_tp)]
    peers += [(at(z, lax.rem(y + d, n_y)), tp) for d in range(1, n_y)]
    peers += [(at(zg * 4 + lax.rem(zl + d, 4), y), tp) for d in range(1, 4)]
    peers += [(at(lax.rem(z + 4 * d, 16), y), tp) for d in range(1, 4)]
    for peer in peers:
        pl.semaphore_signal(barrier, inc=1, device_id=peer, device_id_type=MESH)

    keys = [k_ref[:, h * W : h * W + W] for h in range(2)]
    values = [v_ref[:, h * W : h * W + W] for h in range(2)]
    beta0 = [beta_ref[h : h + 1, :] for h in range(2)]
    beta1 = [beta_ref[2 + h : 3 + h, :] for h in range(2)]
    gates = [gate_ref[h : h + 1, :] for h in range(2)]

    pl.semaphore_wait(barrier, len(peers))

    def w_columns(owner):
        return w_ref.at[:, pl.ds(pl.multiple_of(owner * wide, wide), wide)]

    w_copies = []
    for d in (4, 3, 5, 2, 6, 7, 1):
        owner = lax.rem(tp + d, n_tp)
        copy = pltpu.make_async_remote_copy(
            w_columns(owner), w_buf.at[tp], w_ssem.at[d], w_rsem.at[d], (ctx, owner), MESH
        )
        copy.start()
        w_copies.append(copy)
    w_own = pltpu.make_async_copy(w_columns(tp), w_buf.at[tp], w_lsem)
    w_own.start()

    made = local_maps(keys, values, beta0, beta1, gates)

    def y_copy(j):
        owner = 2 * core + j
        return pltpu.make_async_remote_copy(
            y_send.at[j], y_recv.at[y], y_ssem.at[j], y_rsem.at[y], (at(z, owner), tp), MESH
        )

    for j in range(2):
        move = split2(made[j][0])
        offset = made[j][1].astype(BF16)

        @pl.when(y == 2 * core + j)
        def _():
            y_recv[y, 0] = move[0]
            y_recv[y, 1] = move[1]
            y_recv[y, 2] = offset

        @pl.when(y != 2 * core + j)
        def _():
            y_send[j, 0] = move[0]
            y_send[j, 1] = move[1]
            y_send[j, 2] = offset
            y_copy(j).start()

    for j in range(2):
        eff, loc = local_reads(q_ref[:, j * W : j * W + W], keys[j], made[j])
        hi, lo = split2(eff)
        q_eff[j, :, :W] = hi
        q_eff[j, :, W:] = lo
        o_loc[j] = loc

    def s_copy(target, j):
        return pltpu.make_async_remote_copy(
            s_send.at[target], s_recv.at[j], s_ssem.at[target], s_rsem.at[j],
            (at(z, target), tp), MESH,
        )

    def l_copy(d):
        other = lax.rem(zl + d, 4)
        return pltpu.make_async_remote_copy(
            l_send, l_recv.at[zl], l_ssem.at[d], l_rsem.at[zl], (at(zg * 4 + other, y), tp), MESH
        )

    def h_copy(d):
        return pltpu.make_async_remote_copy(
            h_send, h_recv.at[zg], h_ssem.at[d], h_rsem.at[zg],
            (at(lax.rem(z + 4 * d, 16), y), tp), MESH,
        )

    mine = lax.rem(y, 2)

    @pl.when(y // 2 == core)
    def _():
        for s in range(n_y):

            @pl.when(s != y)
            def _():
                pltpu.make_async_remote_copy(
                    y_recv.at[s], y_recv.at[s], y_ssem.at[0], y_rsem.at[s],
                    (at(z, s), tp), MESH,
                ).wait_recv()

        part = [
            ((y_recv[s, 0], y_recv[s, 1]), y_recv[s, 2].astype(F32)) for s in range(n_y)
        ]
        first_two = compose(part[1], part[0])
        last_two = compose(part[3], part[2])
        whole = compose(last_two, first_two)
        l_send[0] = whole[0][0]
        l_send[1] = whole[1].astype(BF16)
        for d in (3, 1, 2):
            l_copy(d).start()
        l_recv[zl, 0] = whole[0][0]
        l_recv[zl, 1] = whole[1].astype(BF16)
        three = compose(part[2], first_two)
        row = iota((W, W), 0)
        col = iota((W, W), 1)
        eye = (row == col).astype(F32)
        for d in range(1, 4):
            src = lax.rem(zl + d, 4)
            pltpu.make_async_remote_copy(
                l_recv.at[src], l_recv.at[src], l_ssem.at[d], l_rsem.at[src],
                (at(zg * 4 + src, y), tp), MESH,
            ).wait_recv()
        none = jnp.zeros((W, W), BF16)
        grp = [((l_recv[s, 0], none), l_recv[s, 1].astype(F32)) for s in range(4)]
        low_two = compose(grp[1], grp[0])
        high_two = compose(grp[3], grp[2])
        total = compose(high_two, low_two)
        h_send[0] = total[0][0]
        h_send[1] = total[1].astype(BF16)
        for d in (2, 3, 1):

            @pl.when(zg + d < 4)
            def _():
                h_copy(d).start()

        low_three = compose(grp[2], low_two)
        entry_m = jnp.where(
            zl == 0,
            eye,
            jnp.where(
                zl == 1,
                grp[0][0][0].astype(F32),
                jnp.where(
                    zl == 2,
                    low_two[0][0].astype(F32) + low_two[0][1].astype(F32),
                    low_three[0][0].astype(F32) + low_three[0][1].astype(F32),
                ),
            ),
        )
        entry_n = jnp.where(
            zl == 0,
            0.0,
            jnp.where(zl == 1, grp[0][1], jnp.where(zl == 2, low_two[1], low_three[1])),
        )
        entry = (split2(entry_m), entry_n)
        starts = [entry] + [compose(p, entry) for p in (part[0], first_two, three)]
        for s in range(n_y):
            pre_m[s, :, :W] = starts[s][0][0]
            pre_m[s, :, W:] = starts[s][0][1]
            pre_n[s] = starts[s][1]
        state[...] = jnp.zeros((W, W), F32)
        for s in range(3):

            @pl.when(s < zg)
            def _():
                pltpu.make_async_remote_copy(
                    h_recv.at[s], h_recv.at[s], h_ssem.at[0], h_rsem.at[s],
                    (at(z, y), tp), MESH,
                ).wait_recv()
                if s == 0:
                    state[...] = h_recv[s, 1].astype(F32)
                else:
                    now = split2(state[...])
                    state[...] = mm(
                        jnp.concatenate([h_recv[s, 0], h_recv[s, 0]], axis=1),
                        jnp.concatenate([now[0], now[1]], axis=0),
                    ) + h_recv[s, 1].astype(F32)

        now = split2(state[...])
        for s in range(n_y):
            both = pre_m[s]
            moved = mm(both, jnp.concatenate([now[0], now[0]], axis=0)) + mm(both[:, :W], now[1])
            s_send[s] = (moved + pre_n[s]).astype(BF16)
        for d in (2, 1, 3):
            s_copy(lax.rem(y + d, n_y), mine).start()
        s_recv[mine] = s_send[y]

    for j in range(2):

        @pl.when(y != 2 * core + j)
        def _():
            pltpu.make_async_remote_copy(
                s_recv.at[j], s_recv.at[j], s_ssem.at[0], s_rsem.at[j],
                (at(z, 2 * core + j), tp), MESH,
            ).wait_recv()

        entering = s_recv[j]
        out = mm(q_eff[j], jnp.concatenate([entering, entering], axis=0)) + o_loc[j]
        scale = lax.rsqrt(jnp.mean(out * out, axis=1, keepdims=True) + 1e-06)
        gain = gain_ref[:, j * W : j * W + W]
        n_buf[tp, :, j * W : j * W + W] = (out * scale * gain).astype(BF16)

    n_copies = []
    for d in (4, 3, 5, 2, 6, 7, 1):
        other = lax.rem(tp + d, n_tp)
        copy = pltpu.make_async_remote_copy(
            n_buf.at[tp], n_buf.at[tp], n_ssem.at[d], n_rsem.at[d], (ctx, other), MESH
        )
        copy.start()
        n_copies.append(copy)
    w_own.wait()
    total = mm(n_buf[tp], w_buf[tp])
    for d in (1, 7, 2, 6, 3, 5, 4):
        src = lax.rem(tp + n_tp - d, n_tp)
        for buf, ssem, rsem in ((w_buf, w_ssem, w_rsem), (n_buf, n_ssem, n_rsem)):
            pltpu.make_async_remote_copy(
                buf.at[src], buf.at[src], ssem.at[d], rsem.at[d], (ctx, src), MESH
            ).wait_recv()
        total = total + mm(n_buf[src], w_buf[src])
    o_ref[...] = total.astype(BF16)

    for copy in w_copies + n_copies:
        copy.wait_send()
    for j in range(2):

        @pl.when(y != 2 * core + j)
        def _():
            y_copy(j).wait_send()

    @pl.when(y // 2 == core)
    def _():
        for d in range(1, 4):
            l_copy(d).wait_send()

            @pl.when(zg + d < 4)
            def _():
                h_copy(d).wait_send()

            s_copy(lax.rem(y + d, n_y), mine).wait_send()


def local(queries, key_vectors, value_vectors, strengths, log_gate, out_gain, out_weight):
    tokens = queries.shape[0]
    n_tp = 8
    n_y = 4
    width = out_weight.shape[1] // n_tp
    vmem = pl.BlockSpec(memory_space=pltpu.VMEM)
    dma = pltpu.SemaphoreType.DMA
    return pl.pallas_call(
        functools.partial(kernel, n_y, n_tp),
        out_shape=jax.ShapeDtypeStruct((tokens, width), BF16),
        in_specs=[vmem] * 6 + [pl.BlockSpec(memory_space=pl.ANY)],
        out_specs=vmem,
        scratch_shapes=[
            pltpu.VMEM((n_tp, 2 * W, width), BF16),
            pltpu.VMEM((2, 3, W, W), BF16),
            pltpu.VMEM((n_y, 3, W, W), BF16),
            pltpu.VMEM((2, W, W), BF16),
            pltpu.VMEM((4, 2, W, W), BF16),
            pltpu.VMEM((2, W, W), BF16),
            pltpu.VMEM((4, 2, W, W), BF16),
            pltpu.VMEM((n_y, W, 2 * W), BF16),
            pltpu.VMEM((n_y, W, W), F32),
            pltpu.VMEM((W, W), F32),
            pltpu.VMEM((n_y, W, W), BF16),
            pltpu.VMEM((2, W, W), BF16),
            pltpu.VMEM((2, W, 2 * W), BF16),
            pltpu.VMEM((2, W, W), F32),
            pltpu.VMEM((n_tp, W, 2 * W), BF16),
            dma((n_tp,)),
            dma((n_tp,)),
            dma,
            dma((2,)),
            dma((n_y,)),
            dma((4,)),
            dma((4,)),
            dma((4,)),
            dma((4,)),
            dma((n_y,)),
            dma((2,)),
            dma((n_tp,)),
            dma((n_tp,)),
        ],
        compiler_params=pltpu.CompilerParams(collective_id=0, has_side_effects=True),
    )(
        queries,
        key_vectors.reshape(2 * tokens, -1),
        value_vectors.reshape(2 * tokens, -1),
        strengths.reshape(4, tokens),
        log_gate,
        out_gain.reshape(1, -1),
        out_weight,
    )


def solution(mesh):
    placed = (
        P("ctx", "tp"),
        P("ctx", None, "tp"),
        P("ctx", None, "tp"),
        P(None, "tp", "ctx"),
        P("tp", "ctx"),
        P("tp"),
        P("tp", None),
    )
    return jax.shard_map(
        local, mesh=mesh, in_specs=placed, out_specs=P("ctx", "tp"), check_vma=False
    )
```

time: 506 us -> 58 us (0.11)
  waiting for transfers between devices: 347 us -> 0 us
  matrix products: 88.3 us -> 0 us
  Pallas kernels: 0 us -> 53 us
  other arithmetic: 44.3 us -> 0 us
  between operations: 13.5 us -> 0.01 us
    all_gather x2 -> x0, waiting for transfers between devices: 305 us -> none  [carried_in(): everything = jax.tree.map(lambda part: lax.all_gather(part, axis), x)]
    dot_general x81 -> x0, matrix products: 87.7 us -> none  [the longest x76 83.8 us: matmul_heads(): jnp.einsum('...ij,...jk->...ik', left_side, right_side, precision=highest)]
    pallas_call x0 -> x1, Pallas kernels: none -> 53 us  [local(): pl.pallas_call(functools.partial(kernel, n_y, n_tp), out_shape=jax.ShapeD...]
    reduce_scatter x1 -> x0, waiting for transfers between devices: 41.1 us -> none  [local(): lax.psum_scatter(terms.astype(jnp.bfloat16), 'tp', scatter_dimension=1, t...]
    another operation x5 -> x0, other arithmetic: 40.1 us -> none  [the longest x4 39.4 us: solve_lower(): jax.scipy.linalg.solve_triangular(system, right_side, lower=True, unit_di...]
  transfers between devices with their start and end apart: 3 -> 0, of which waited for: 3 -> 0; matrix products, arithmetic and copies ran while one was open for 0% -> 0% of each run, Pallas kernels for 0% -> 0%
where the time goes in v1:
time: 58 us; the launch traced here: 57.8 us
  Pallas kernels  53 us (91%)
  local copies, waits for them, and re-layouts  4.78 us (8%)
    pallas_call x1, Pallas kernels, local(): pl.pallas_call(functools.partial(kernel, n_y, n_tp), out_shape=jax.ShapeD...  53 us
    reshape x1, local copies, waits for them, and re-layouts, local(): key_vectors.reshape(2 * tokens, -1)  1.61 us
    reshape x1, local copies, waits for them, and re-layouts, local(): value_vectors.reshape(2 * tokens, -1)  1.6 us
    unnamed x1, local copies, waits for them, and re-layouts  1.57 us

profile of v1, /device:TPU:1, one launch (start us, length us, event | category | flops | bytes accessed | tf_op | source)
XLA Modules:
  0.0 57.8 jit_solution(7122982425550102792)
XLA Ops:
  0.0 1.6 %reshape.12.k_ref = bf16[256,256]{1,0:T(8,128)(2,1)} reshape(bf16[128,2,256]{2,1,0:T(2,128)(2,1)} %param.8) | data formatting | bytes 262144 | tf_op jit(solution)/shard_map/reshape | solution.py:485
  1.6 1.6 %reshape.13.v_ref = bf16[256,256]{1,0:T(8,128)(2,1)} reshape(bf16[128,2,256]{2,1,0:T(2,128)(2,1)} %param.9) | data formatting | bytes 262144 | tf_op jit(solution)/shard_map/reshape | solution.py:486
  3.2 53.0 %shard_map.73 = bf16[128,512]{1,0:T(8,128)(2,1)} custom-call(bf16[128,256]{1,0:T(8,128)(2,1)} %q_ref.1, bf16[256,256]{1,0:T(8,128)(2,1)} %reshape.12.k_ref, bf16[256,256]{1,0:T(8,128)(2,1)} %reshape.13.v_ref, f32[4,128]{1,0:T(4,128)} %bitcast.2, f32[2,128]{1,0:T(2,128)} %gate_ref.1, f32[1,256]{1,0:T(1,128)} %bitcast.3, bf16[256,4096]{1,0:T(8,128)(2,1)} %w_ref.1), custom_call_target="tpu_custom_call" | custom-call | tf_op jit(solution)/shard_map/pallas_call | solution.py:447
  56.2 1.6 %copy.9 = bf16[128,512]{1,0:T(8,128)(2,1)} copy(bf16[128,512]{1,0:T(8,128)(2,1)} %shard_map.73) | data formatting | bytes 262144

commit v2 on v1

--- a/solution.py
+++ b/solution.py
@@ -33,9 +33,16 @@
     return hi, mid, (rest - mid.astype(F32)).astype(BF16)
 
 
+def left3(pair):
+    return jnp.concatenate([pair[0], pair[1], pair[0]], axis=1)
+
+
+def right3(pair):
+    return jnp.concatenate([pair[0], pair[0], pair[1]], axis=0)
+
+
 def dot_pairs(a, b):
-    both = mm(jnp.concatenate([a[0], a[1]], axis=1), jnp.concatenate([b[0], b[0]], axis=0))
-    return both + mm(a[0], b[1])
+    return mm(left3(a), right3(b))
 
 
 def dot_pair_one(a, b):
@@ -46,102 +53,152 @@
     return dot_pairs(split2(a), split2(b))
 
 
-def spread_nt(mask, rows):
-    hi, mid, lo = split3(rows)
-    return mm_nt(mask, hi) + mm_nt(mask, mid) + mm_nt(mask, lo)
-
-
-def spread_rows(rows, mask):
-    hi, mid, lo = split3(rows)
-    return mm_nt(hi, mask) + mm_nt(mid, mask) + mm_nt(lo, mask)
-
-
 def iota(shape, dim):
     return lax.broadcasted_iota(jnp.int32, shape, dim)
 
 
-def local_maps(keys, values, beta0, beta1, gate):
-    heads = len(keys)
+def bits(mask):
+    return mask.astype(F32).astype(BF16)
+
+
+def by_rows(block, rows):
+    n = block.shape[0]
+    return block.reshape(n // 8, 8, W), jnp.broadcast_to(rows[None], (n // 8, 8, W))
+
+
+def times_rows(block, rows):
+    a, b = by_rows(block, rows)
+    return (a * b).reshape(block.shape)
+
+
+def minus_rows(block, rows):
+    a, b = by_rows(block, rows)
+    return (a - b).reshape(block.shape)
+
+
+def make_masks():
     step = iota((2 * W, W), 0)
     token = iota((2 * W, W), 1)
-    upto = (2 * token <= step).astype(F32).astype(BF16)
-    first = (2 * token == step).astype(F32).astype(BF16)
-    second = (2 * token + 1 == step).astype(F32).astype(BF16)
-    ones = jnp.ones((W, W), BF16)
     row = iota((W, W), 0)
     col = iota((W, W), 1)
+    upto = bits(2 * token <= step)
+    first = bits(2 * token == step)
+    second = bits(2 * token + 1 == step)
+    levels = []
+    size = 1
+    while size < W:
+        levels.append(bits((row // size == col // size + 1) & ((row // size) % 2 == 1)))
+        size *= 2
+    return (
+        jnp.concatenate([upto] * 3, axis=1),
+        jnp.concatenate([first] * 3 + [second] * 3, axis=1),
+        levels,
+    )
+
+
+def local_maps(masks, keys, values, beta0, beta1, gate):
+    heads = len(keys)
+    upto3, pick, levels = masks
+    row = iota((W, W), 0)
+    col = iota((W, W), 1)
+    eye = (row == col).astype(F32)
     pre = []
     low = []
     for h in range(heads):
         k = keys[h]
         k32 = k.astype(F32)
-        square = split2(k32 * k32)
-        inv_col = lax.rsqrt(mm(square[0], ones) + mm(square[1], ones) + 1e-06)
-        inv_row = lax.rsqrt(mm_nt(ones, square[0]) + mm_nt(ones, square[1]) + 1e-06)
-        g = jnp.broadcast_to(gate[h], (W, W))
-        c_col = spread_nt(upto, g)
-        c_row = spread_rows(g, upto)
-        beta = spread_nt(first, jnp.broadcast_to(beta0[h], (W, W))) + spread_nt(
-            second, jnp.broadcast_to(beta1[h], (W, W))
-        )
         gram = mm_nt(k, k)
+        inv_col = lax.rsqrt(jnp.sum(k32 * k32, axis=1, keepdims=True) + 1e-06)
+        inv_row = []
+        for a in range(2):
+            part = jnp.where(row == col, gram[a * W : a * W + W, a * W : a * W + W], 0.0)
+            total = jnp.sum(part.reshape(W // 8, 8, W), axis=0)
+            total = jnp.broadcast_to(jnp.sum(total, axis=0, keepdims=True), (8, W))
+            inv_row.append(lax.rsqrt(total + 1e-06))
+        g3 = jnp.concatenate(split3(jnp.broadcast_to(gate[h], (W, W))), axis=1)
+        b3 = jnp.concatenate(
+            split3(jnp.broadcast_to(beta0[h], (W, W))) + split3(jnp.broadcast_to(beta1[h], (W, W))),
+            axis=1,
+        )
+        c_col = mm_nt(upto3, g3)
+        c_row = mm_nt(g3[:8], upto3)
+        beta = mm_nt(pick, b3)
+        beta_row = mm_nt(b3[:8], pick)
+        grow_row = jnp.exp(c_row)
         scaled = beta * inv_col
         blocks = {}
         for a, b in ((0, 0), (1, 1), (1, 0)):
             ra, cb = slice(a * W, a * W + W), slice(b * W, b * W + W)
-            diff = c_col[ra] - c_row[:, cb]
+            diff = minus_rows(c_col[ra], c_row[:, cb])
             if a == b:
                 diff = jnp.where(row > col, diff, -1e30)
-            blocks[a, b] = scaled[ra] * jnp.exp(diff) * inv_row[:, cb] * gram[ra, cb]
-        grow = jnp.exp(c_col)
-        right = jnp.concatenate(
-            [scaled * grow * k32, beta * values[h].astype(F32)], axis=1
-        )
+            block = scaled[ra] * jnp.exp(diff) * times_rows(gram[ra, cb], inv_row[b])
+            blocks[a, b] = split2(block)
         last = c_col[2 * W - 1 : 2 * W]
         tail = inv_col * jnp.exp(last - c_col)
-        pre.append((blocks[1, 0], right, tail, jnp.exp(last), c_row, inv_row, g))
+        pre.append((blocks[1, 0], beta_row, grow_row, inv_row, tail, jnp.exp(last), c_row, g3))
         low += [blocks[0, 0], blocks[1, 1]]
-    eye = (row == col).astype(F32)
     inverse = [
-        eye - jnp.where((row == col + 1) & (row % 2 == 1), part, 0.0) for part in low
+        eye - (part[0] * levels[0]).astype(F32) - (part[1] * levels[0]).astype(F32) for part in low
     ]
-    size = 2
-    while size < W:
-        mask = (row // size == col // size + 1) & ((row // size) % 2 == 1)
+    for mask in levels[1:]:
         pairs = [split2(t) for t in inverse]
         inner = [
-            dot_pairs(split2(jnp.where(mask, part, 0.0)), pair) for part, pair in zip(low, pairs)
+            dot_pairs((part[0] * mask, part[1] * mask), pair) for part, pair in zip(low, pairs)
         ]
-        inverse = [
-            t - dot_pairs(pair, split2(c)) for t, pair, c in zip(inverse, pairs, inner)
-        ]
-        size *= 2
+        inverse = [t - dot_pairs(pair, split2(c)) for t, pair, c in zip(inverse, pairs, inner)]
     out = []
+    pairs = [split2(t) for t in inverse]
+    inner = [dot_pairs(pre[h][0], pairs[2 * h]) for h in range(heads)]
+    below = [dot_pairs(pairs[2 * h + 1], split2(inner[h])) for h in range(heads)]
     for h in range(heads):
-        below, right, tail, decay, c_row, inv_row, g = pre[h]
-        top = x3(inverse[2 * h], right[:W])
-        bottom = x3(inverse[2 * h + 1], right[W:] - x3(below, top))
-        write = jnp.concatenate([top, bottom], axis=0)
+        _, beta_row, grow_row, inv_row, tail, decay, c_row, g3 = pre[h]
+        top = []
+        bottom = []
+        for which, data in ((0, keys[h]), (1, values[h])):
+            scale = [beta_row[:, a * W : a * W + W] for a in range(2)]
+            if which == 0:
+                scale = [
+                    scale[a] * grow_row[:, a * W : a * W + W] * inv_row[a] for a in range(2)
+                ]
+            t00 = split2(times_rows(inverse[2 * h], scale[0]))
+            t10 = split2(times_rows(below[h], -scale[0]))
+            t11 = split2(times_rows(inverse[2 * h + 1], scale[1]))
+            d0, d1 = data[:W], data[W:]
+            top.append(
+                mm(jnp.concatenate(t00, axis=1), jnp.concatenate([d0, d0], axis=0))
+            )
+            bottom.append(
+                mm(
+                    jnp.concatenate([t10[0], t11[0], t10[1], t11[1]], axis=1),
+                    jnp.concatenate([d0, d1, d0, d1], axis=0),
+                )
+            )
+        write = jnp.concatenate(
+            [jnp.concatenate(top, axis=1), jnp.concatenate(bottom, axis=1)], axis=0
+        )
         turned = keys[h].astype(F32).T.astype(BF16)
         weighted = split2(jnp.concatenate([tail, tail], axis=1) * write)
-        both = mm(turned, weighted[0]) + mm(turned, weighted[1])
+        both = mm(jnp.concatenate([turned, turned], axis=1), jnp.concatenate(weighted, axis=0))
         move = jnp.where(row == col, decay, 0.0) - both[:, :W]
-        out.append((move, both[:, W:], write, c_row, inv_row, g))
+        out.append((move, both[:, W:], write, c_row, inv_row, g3))
     return out
 
 
 def local_reads(query, key, made):
-    _, _, write, c_row, inv_row, g = made
+    _, _, write, c_row, inv_row, g3 = made
     row = iota((W, W), 0)
     col = iota((W, W), 1)
-    upto = (col <= row).astype(F32).astype(BF16)
-    c_tok = spread_nt(upto, g)
-    t = iota((W, 2 * W), 0)
-    m = iota((W, 2 * W), 1)
-    diff = jnp.concatenate([c_tok, c_tok], axis=1) - c_row
-    ratio = jnp.exp(jnp.where(m <= 2 * t + 1, diff, -1e30))
-    weights = ratio * inv_row * mm_nt(query, key)
-    both = x3(weights, write)
+    upto = bits(col <= row)
+    c_tok = mm_nt(jnp.concatenate([upto] * 3, axis=1), g3)
+    seen = mm_nt(query, key)
+    weights = []
+    for a in range(2):
+        cols = slice(a * W, a * W + W)
+        diff = minus_rows(c_tok, c_row[:, cols])
+        ratio = jnp.exp(jnp.where(col + a * W <= 2 * row + 1, diff, -1e30))
+        weights.append(ratio * times_rows(seen[:, cols], inv_row[a]))
+    both = x3(jnp.concatenate(weights, axis=1), write)
     return jnp.exp(c_tok) * query.astype(F32) - both[:, :W], both[:, W:]
 
 
@@ -162,6 +219,8 @@
     gain_ref,
     w_ref,
     o_ref,
+    k_buf,
+    v_buf,
     w_buf,
     y_send,
     y_recv,
@@ -190,6 +249,9 @@
     s_rsem,
     n_ssem,
     n_rsem,
+    f_ssem,
+    i_sem,
+    ready,
 ):
     ctx = lax.axis_index("ctx")
     tp = lax.axis_index("tp")
@@ -203,21 +265,47 @@
     def at(zz, yy):
         return zz * n_y + yy
 
+    loads = []
+    for i, (ref, buf) in enumerate(((k_ref, k_buf), (v_ref, v_buf))):
+        for h in range(2):
+            copy = pltpu.make_async_copy(
+                ref.reshape(2 * W, 2 * W).at[:, pl.ds(h * W, W)], buf.at[h], i_sem.at[2 * i + h]
+            )
+            copy.start()
+            loads.append(copy)
+
     barrier = pltpu.get_barrier_semaphore()
-    peers = [(ctx, lax.rem(tp + d, n_tp)) for d in range(1, n_tp)]
-    peers += [(at(z, lax.rem(y + d, n_y)), tp) for d in range(1, n_y)]
-    peers += [(at(zg * 4 + lax.rem(zl + d, 4), y), tp) for d in range(1, 4)]
-    peers += [(at(lax.rem(z + 4 * d, 16), y), tp) for d in range(1, 4)]
-    for peer in peers:
+    near = [(ctx, lax.rem(tp + d, n_tp)) for d in range(1, n_tp)]
+    near += [(at(z, lax.rem(y + d, n_y)), tp) for d in range(1, n_y)]
+    near += [(at(zg * 4 + lax.rem(zl + d, 4), y), tp) for d in range(1, 4)]
+    for peer in near:
         pl.semaphore_signal(barrier, inc=1, device_id=peer, device_id_type=MESH)
-
-    keys = [k_ref[:, h * W : h * W + W] for h in range(2)]
-    values = [v_ref[:, h * W : h * W + W] for h in range(2)]
+    for d in range(1, 4):
+
+        @pl.when(zg + d < 4)
+        def _():
+            pl.semaphore_signal(
+                barrier, inc=1, device_id=(at(lax.rem(z + 4 * d, 16), y), tp), device_id_type=MESH
+            )
+
+    masks = make_masks()
+    for copy in loads:
+        copy.wait()
+    keys = [k_buf[h] for h in range(2)]
+    values = [v_buf[h] for h in range(2)]
     beta0 = [beta_ref[h : h + 1, :] for h in range(2)]
     beta1 = [beta_ref[2 + h : 3 + h, :] for h in range(2)]
     gates = [gate_ref[h : h + 1, :] for h in range(2)]
 
-    pl.semaphore_wait(barrier, len(peers))
+    pl.semaphore_wait(barrier, len(near) + zg)
+    for d in range(1, 4):
+
+        @pl.when(zg - d >= 0)
+        def _():
+            pl.semaphore_signal(
+                ready, inc=1, device_id=(at(lax.rem(z + 16 - 4 * d, 16), y), tp),
+                device_id_type=MESH,
+            )
 
     def w_columns(owner):
         return w_ref.at[:, pl.ds(pl.multiple_of(owner * wide, wide), wide)]
@@ -226,14 +314,14 @@
     for d in (4, 3, 5, 2, 6, 7, 1):
         owner = lax.rem(tp + d, n_tp)
         copy = pltpu.make_async_remote_copy(
-            w_columns(owner), w_buf.at[tp], w_ssem.at[d], w_rsem.at[d], (ctx, owner), MESH
+            w_columns(owner), w_buf.at[tp], w_ssem.at[d], w_rsem.at[tp], (ctx, owner), MESH
         )
         copy.start()
         w_copies.append(copy)
     w_own = pltpu.make_async_copy(w_columns(tp), w_buf.at[tp], w_lsem)
     w_own.start()
 
-    made = local_maps(keys, values, beta0, beta1, gates)
+    made = local_maps(masks, keys, values, beta0, beta1, gates)
 
     def y_copy(j):
         owner = 2 * core + j
@@ -284,6 +372,15 @@
         )
 
     mine = lax.rem(y, 2)
+
+    def ready_wait():
+        @pl.when(zg < 3)
+        def _():
+            pl.semaphore_wait(ready, 3 - zg)
+
+    @pl.when(y // 2 != core)
+    def _():
+        ready_wait()
 
     @pl.when(y // 2 == core)
     def _():
@@ -325,6 +422,7 @@
         total = compose(high_two, low_two)
         h_send[0] = total[0][0]
         h_send[1] = total[1].astype(BF16)
+        ready_wait()
         for d in (2, 3, 1):
 
             @pl.when(zg + d < 4)
@@ -398,27 +496,58 @@
         gain = gain_ref[:, j * W : j * W + W]
         n_buf[tp, :, j * W : j * W + W] = (out * scale * gain).astype(BF16)
 
-    n_copies = []
-    for d in (4, 3, 5, 2, 6, 7, 1):
-        other = lax.rem(tp + d, n_tp)
-        copy = pltpu.make_async_remote_copy(
-            n_buf.at[tp], n_buf.at[tp], n_ssem.at[d], n_rsem.at[d], (ctx, other), MESH
-        )
-        copy.start()
-        n_copies.append(copy)
+    chip = tp // 2
+    partner = chip * 2 + 1 - core
+
+    def n_copy(d):
+        other = lax.rem(chip + d, 4) * 2 + core
+        return pltpu.make_async_remote_copy(
+            n_buf.at[tp], n_buf.at[tp], n_ssem.at[d], n_rsem.at[tp], (ctx, other), MESH
+        )
+
+    def pass_on(d):
+        src = lax.rem(chip + d, 4) * 2 + core
+        return pltpu.make_async_remote_copy(
+            n_buf.at[src], n_buf.at[src], f_ssem.at[d], n_rsem.at[src], (ctx, partner), MESH
+        )
+
+    def arrived(src):
+        pltpu.make_async_remote_copy(
+            n_buf.at[src], n_buf.at[src], f_ssem.at[0], n_rsem.at[src], (ctx, partner), MESH
+        ).wait_recv()
+
+    def w_arrived(src):
+        pltpu.make_async_remote_copy(
+            w_buf.at[src], w_buf.at[src], w_ssem.at[0], w_rsem.at[src], (ctx, partner), MESH
+        ).wait_recv()
+
+    for d in (2, 1, 3):
+        n_copy(d).start()
+    pass_on(0).start()
     w_own.wait()
     total = mm(n_buf[tp], w_buf[tp])
-    for d in (1, 7, 2, 6, 3, 5, 4):
-        src = lax.rem(tp + n_tp - d, n_tp)
-        for buf, ssem, rsem in ((w_buf, w_ssem, w_rsem), (n_buf, n_ssem, n_rsem)):
-            pltpu.make_async_remote_copy(
-                buf.at[src], buf.at[src], ssem.at[d], rsem.at[d], (ctx, src), MESH
-            ).wait_recv()
+    w_arrived(partner)
+    arrived(partner)
+    total = total + mm(n_buf[partner], w_buf[partner])
+    for d in (1, 3, 2):
+        src = lax.rem(chip + d, 4) * 2 + core
+        arrived(src)
+        pass_on(d).start()
+        w_arrived(src)
+        total = total + mm(n_buf[src], w_buf[src])
+    for d in (1, 3, 2):
+        src = lax.rem(chip + d, 4) * 2 + 1 - core
+        w_arrived(src)
+        arrived(src)
         total = total + mm(n_buf[src], w_buf[src])
     o_ref[...] = total.astype(BF16)
 
-    for copy in w_copies + n_copies:
+    for copy in w_copies:
         copy.wait_send()
+    for d in range(4):
+        pass_on(d).wait_send()
+    for d in range(1, 4):
+        n_copy(d).wait_send()
     for j in range(2):
 
         @pl.when(y != 2 * core + j)
@@ -443,13 +572,16 @@
     n_y = 4
     width = out_weight.shape[1] // n_tp
     vmem = pl.BlockSpec(memory_space=pltpu.VMEM)
+    hbm = pl.BlockSpec(memory_space=pl.ANY)
     dma = pltpu.SemaphoreType.DMA
     return pl.pallas_call(
         functools.partial(kernel, n_y, n_tp),
         out_shape=jax.ShapeDtypeStruct((tokens, width), BF16),
-        in_specs=[vmem] * 6 + [pl.BlockSpec(memory_space=pl.ANY)],
+        in_specs=[vmem, hbm, hbm, vmem, vmem, vmem, hbm],
         out_specs=vmem,
         scratch_shapes=[
+            pltpu.VMEM((2, 2 * W, W), BF16),
+            pltpu.VMEM((2, 2 * W, W), BF16),
             pltpu.VMEM((n_tp, 2 * W, width), BF16),
             pltpu.VMEM((2, 3, W, W), BF16),
             pltpu.VMEM((n_y, 3, W, W), BF16),
@@ -476,14 +608,17 @@
             dma((4,)),
             dma((n_y,)),
             dma((2,)),
+            dma((4,)),
             dma((n_tp,)),
-            dma((n_tp,)),
+            dma((4,)),
+            dma((4,)),
+            pltpu.SemaphoreType.REGULAR,
         ],
         compiler_params=pltpu.CompilerParams(collective_id=0, has_side_effects=True),
     )(
         queries,
-        key_vectors.reshape(2 * tokens, -1),
-        value_vectors.reshape(2 * tokens, -1),
+        key_vectors,
+        value_vectors,
         strengths.reshape(4, tokens),
         log_gate,
         out_gain.reshape(1, -1),

time: 58 us -> 45.7 us (0.79)
  Pallas kernels: 53 us -> 43.9 us
  local copies, waits for them, and re-layouts: 4.78 us -> 1.57 us
    pallas_call x1, Pallas kernels: 53 us -> 43.9 us  [local(): pl.pallas_call(functools.partial(kernel, n_y, n_tp), out_shape=jax.ShapeD...]
    reshape x2 -> x0, local copies, waits for them, and re-layouts: 3.21 us -> none  [the longest x1 1.61 us: local(): key_vectors.reshape(2 * tokens, -1)]
where the time goes in v2:
time: 45.7 us; the launch traced here: 45.5 us
  Pallas kernels  43.9 us (96%)
  local copies, waits for them, and re-layouts  1.57 us (3%)
    pallas_call x1, Pallas kernels, local(): pl.pallas_call(functools.partial(kernel, n_y, n_tp), out_shape=jax.ShapeD...  43.9 us
    unnamed x1, local copies, waits for them, and re-layouts  1.57 us

profile of v2, /device:TPU:1, one launch (start us, length us, event | category | flops | bytes accessed | tf_op | source)
XLA Modules:
  0.0 45.5 jit_solution(17153369975164109052)
XLA Ops:
  0.0 43.9 %shard_map.73 = bf16[128,512]{1,0:T(8,128)(2,1)} custom-call(bf16[128,256]{1,0:T(8,128)(2,1)} %q_ref.1, bf16[128,2,256]{2,1,0:T(2,128)(2,1)} %k_ref.1, bf16[128,2,256]{2,1,0:T(2,128)(2,1)} %v_ref.1, f32[4,128]{1,0:T(4,128)} %bitcast.2, f32[2,128]{1,0:T(2,128)} %gate_ref.1, f32[1,256]{1,0:T(1,128)} %bitcast.3, bf16[256,4096]{1,0:T(8,128)(2,1)} %w_ref.1), custom_call_target="tpu_custom_call" | custom-call | tf_op jit(solution)/shard_map/pallas_call | solution.py:577
  43.9 1.6 %copy.9 = bf16[128,512]{1,0:T(8,128)(2,1)} copy(bf16[128,512]{1,0:T(8,128)(2,1)} %shard_map.73) | data formatting | bytes 262144

commit v3 on v2

--- a/solution.py
+++ b/solution.py
@@ -231,10 +231,9 @@
     pre_m,
     pre_n,
     state,
-    s_send,
-    s_recv,
-    q_eff,
-    o_loc,
+    r_send,
+    r_recv,
+    n_send,
     n_buf,
     w_ssem,
     w_rsem,
@@ -245,8 +244,8 @@
     l_rsem,
     h_ssem,
     h_rsem,
-    s_ssem,
-    s_rsem,
+    r_ssem,
+    r_rsem,
     n_ssem,
     n_rsem,
     f_ssem,
@@ -276,7 +275,9 @@
 
     barrier = pltpu.get_barrier_semaphore()
     near = [(ctx, lax.rem(tp + d, n_tp)) for d in range(1, n_tp)]
-    near += [(at(z, lax.rem(y + d, n_y)), tp) for d in range(1, n_y)]
+    near += [
+        (at(z, lax.rem(y + d, n_y)), lax.rem(tp + 2 * e, n_tp)) for d in range(1, n_y) for e in range(4)
+    ]
     near += [(at(zg * 4 + lax.rem(zl + d, 4), y), tp) for d in range(1, 4)]
     for peer in near:
         pl.semaphore_signal(barrier, inc=1, device_id=peer, device_id_type=MESH)
@@ -311,8 +312,9 @@
         return w_ref.at[:, pl.ds(pl.multiple_of(owner * wide, wide), wide)]
 
     w_copies = []
-    for d in (4, 3, 5, 2, 6, 7, 1):
-        owner = lax.rem(tp + d, n_tp)
+    for d, flip in ((2, 0), (2, 1), (1, 0), (3, 0), (1, 1), (3, 1), (0, 1)):
+        owner = lax.rem(tp // 2 + d, 4) * 2 + lax.rem(core + flip, 2)
+        d = 2 * d + flip
         copy = pltpu.make_async_remote_copy(
             w_columns(owner), w_buf.at[tp], w_ssem.at[d], w_rsem.at[tp], (ctx, owner), MESH
         )
@@ -321,43 +323,53 @@
     w_own = pltpu.make_async_copy(w_columns(tp), w_buf.at[tp], w_lsem)
     w_own.start()
 
-    made = local_maps(masks, keys, values, beta0, beta1, gates)
-
     def y_copy(j):
         owner = 2 * core + j
         return pltpu.make_async_remote_copy(
             y_send.at[j], y_recv.at[y], y_ssem.at[j], y_rsem.at[y], (at(z, owner), tp), MESH
         )
 
-    for j in range(2):
-        move = split2(made[j][0])
-        offset = made[j][1].astype(BF16)
-
-        @pl.when(y == 2 * core + j)
-        def _():
-            y_recv[y, 0] = move[0]
-            y_recv[y, 1] = move[1]
-            y_recv[y, 2] = offset
-
-        @pl.when(y != 2 * core + j)
-        def _():
-            y_send[j, 0] = move[0]
-            y_send[j, 1] = move[1]
-            y_send[j, 2] = offset
-            y_copy(j).start()
-
-    for j in range(2):
-        eff, loc = local_reads(q_ref[:, j * W : j * W + W], keys[j], made[j])
-        hi, lo = split2(eff)
-        q_eff[j, :, :W] = hi
-        q_eff[j, :, W:] = lo
-        o_loc[j] = loc
-
-    def s_copy(target, j):
+    def r_copy(j):
+        owner = 2 * core + j
         return pltpu.make_async_remote_copy(
-            s_send.at[target], s_recv.at[j], s_ssem.at[target], s_rsem.at[j],
-            (at(z, target), tp), MESH,
-        )
+            r_send.at[j], r_recv.at[y], r_ssem.at[j], r_rsem.at[y], (at(z, owner), tp), MESH
+        )
+
+    @pl.when(tp >= 0)
+    def _():
+        made = local_maps(masks, keys, values, beta0, beta1, gates)
+        for j in range(2):
+            move = split2(made[j][0])
+            offset = made[j][1].astype(BF16)
+
+            @pl.when(y == 2 * core + j)
+            def _():
+                y_recv[y, 0] = move[0]
+                y_recv[y, 1] = move[1]
+                y_recv[y, 2] = offset
+
+            @pl.when(y != 2 * core + j)
+            def _():
+                y_send[j, 0] = move[0]
+                y_send[j, 1] = move[1]
+                y_send[j, 2] = offset
+                y_copy(j).start()
+
+        for j in range(2):
+            eff, loc = local_reads(q_ref[:, j * W : j * W + W], keys[j], made[j])
+            eff = eff.astype(BF16)
+            loc = loc.astype(BF16)
+
+            @pl.when(y == 2 * core + j)
+            def _():
+                r_recv[y, 0] = eff
+                r_recv[y, 1] = loc
+
+            @pl.when(y != 2 * core + j)
+            def _():
+                r_send[j, 0] = eff
+                r_send[j, 1] = loc
+                r_copy(j).start()
 
     def l_copy(d):
         other = lax.rem(zl + d, 4)
@@ -371,7 +383,22 @@
             (at(lax.rem(z + 4 * d, 16), y), tp), MESH,
         )
 
-    mine = lax.rem(y, 2)
+    def h_copy_first(d):
+        return pltpu.make_async_remote_copy(
+            h_send.at[1], h_recv.at[0, 1], h_ssem.at[d], h_rsem.at[0],
+            (at(lax.rem(z + 4 * d, 16), y), tp), MESH,
+        )
+
+    chip = tp // 2
+    partner = chip * 2 + 1 - core
+
+    def n_copy(dy, dx):
+        s = lax.rem(y + dy, n_y)
+        other = lax.rem(chip + dx, 4) * 2 + core
+        return pltpu.make_async_remote_copy(
+            n_send.at[s], n_buf.at[chip * 4 + y], n_ssem.at[dy * 4 + dx],
+            n_rsem.at[chip * 4 + y], (at(z, s), other), MESH,
+        )
 
     def ready_wait():
         @pl.when(zg < 3)
@@ -405,10 +432,6 @@
             l_copy(d).start()
         l_recv[zl, 0] = whole[0][0]
         l_recv[zl, 1] = whole[1].astype(BF16)
-        three = compose(part[2], first_two)
-        row = iota((W, W), 0)
-        col = iota((W, W), 1)
-        eye = (row == col).astype(F32)
         for d in range(1, 4):
             src = lax.rem(zl + d, 4)
             pltpu.make_async_remote_copy(
@@ -423,97 +446,110 @@
         h_send[0] = total[0][0]
         h_send[1] = total[1].astype(BF16)
         ready_wait()
-        for d in (2, 3, 1):
-
-            @pl.when(zg + d < 4)
+        @pl.when(zg == 0)
+        def _():
+            for d in (2, 3, 1):
+                h_copy_first(d).start()
+
+        for d in (2, 1):
+
+            @pl.when((zg > 0) & (zg + d < 4))
             def _():
                 h_copy(d).start()
 
-        low_three = compose(grp[2], low_two)
-        entry_m = jnp.where(
-            zl == 0,
-            eye,
-            jnp.where(
-                zl == 1,
-                grp[0][0][0].astype(F32),
+        @pl.when(tp >= 0)
+        def _():
+            row = iota((W, W), 0)
+            col = iota((W, W), 1)
+            eye = (row == col).astype(F32)
+            three = compose(part[2], first_two)
+            low_three = compose(grp[2], low_two)
+
+            def joined(pair):
+                return pair[0].astype(F32) + pair[1].astype(F32)
+
+            entry_m = jnp.where(
+                zl == 0,
+                eye,
                 jnp.where(
-                    zl == 2,
-                    low_two[0][0].astype(F32) + low_two[0][1].astype(F32),
-                    low_three[0][0].astype(F32) + low_three[0][1].astype(F32),
+                    zl == 1,
+                    grp[0][0][0].astype(F32),
+                    jnp.where(zl == 2, joined(low_two[0]), joined(low_three[0])),
                 ),
-            ),
-        )
-        entry_n = jnp.where(
-            zl == 0,
-            0.0,
-            jnp.where(zl == 1, grp[0][1], jnp.where(zl == 2, low_two[1], low_three[1])),
-        )
-        entry = (split2(entry_m), entry_n)
-        starts = [entry] + [compose(p, entry) for p in (part[0], first_two, three)]
-        for s in range(n_y):
-            pre_m[s, :, :W] = starts[s][0][0]
-            pre_m[s, :, W:] = starts[s][0][1]
-            pre_n[s] = starts[s][1]
-        state[...] = jnp.zeros((W, W), F32)
+            )
+            entry_n = jnp.where(
+                zl == 0,
+                0.0,
+                jnp.where(zl == 1, grp[0][1], jnp.where(zl == 2, low_two[1], low_three[1])),
+            )
+            entry = (split2(entry_m), entry_n)
+            starts = [entry] + [compose(p, entry) for p in (part[0], first_two, three)]
+            for s in range(n_y):
+
+                @pl.when(s != y)
+                def _():
+                    pltpu.make_async_remote_copy(
+                        r_recv.at[s], r_recv.at[s], r_ssem.at[0], r_rsem.at[s],
+                        (at(z, s), tp), MESH,
+                    ).wait_recv()
+
+            for s in range(n_y):
+                read = r_recv[s, 0]
+                twice = jnp.concatenate([read, read], axis=1)
+                move = split2(mm(twice, jnp.concatenate(starts[s][0], axis=0)))
+                pre_m[s] = left3(move)
+                pre_n[s] = mm(
+                    twice, jnp.concatenate(split2(starts[s][1]), axis=0)
+                ) + r_recv[s, 1].astype(F32)
+            state[...] = jnp.zeros((W, W), F32)
+
         for s in range(3):
 
             @pl.when(s < zg)
             def _():
-                pltpu.make_async_remote_copy(
-                    h_recv.at[s], h_recv.at[s], h_ssem.at[0], h_rsem.at[s],
-                    (at(z, y), tp), MESH,
-                ).wait_recv()
                 if s == 0:
-                    state[...] = h_recv[s, 1].astype(F32)
+                    pltpu.make_async_remote_copy(
+                        h_recv.at[0, 1], h_recv.at[0, 1], h_ssem.at[0], h_rsem.at[0],
+                        (at(z, y), tp), MESH,
+                    ).wait_recv()
+                    state[...] = h_recv[0, 1].astype(F32)
                 else:
+                    pltpu.make_async_remote_copy(
+                        h_recv.at[s], h_recv.at[s], h_ssem.at[0], h_rsem.at[s],
+                        (at(z, y), tp), MESH,
+                    ).wait_recv()
                     now = split2(state[...])
                     state[...] = mm(
                         jnp.concatenate([h_recv[s, 0], h_recv[s, 0]], axis=1),
                         jnp.concatenate([now[0], now[1]], axis=0),
                     ) + h_recv[s, 1].astype(F32)
 
-        now = split2(state[...])
-        for s in range(n_y):
-            both = pre_m[s]
-            moved = mm(both, jnp.concatenate([now[0], now[0]], axis=0)) + mm(both[:, :W], now[1])
-            s_send[s] = (moved + pre_n[s]).astype(BF16)
-        for d in (2, 1, 3):
-            s_copy(lax.rem(y + d, n_y), mine).start()
-        s_recv[mine] = s_send[y]
-
-    for j in range(2):
-
-        @pl.when(y != 2 * core + j)
-        def _():
-            pltpu.make_async_remote_copy(
-                s_recv.at[j], s_recv.at[j], s_ssem.at[0], s_rsem.at[j],
-                (at(z, 2 * core + j), tp), MESH,
-            ).wait_recv()
-
-        entering = s_recv[j]
-        out = mm(q_eff[j], jnp.concatenate([entering, entering], axis=0)) + o_loc[j]
-        scale = lax.rsqrt(jnp.mean(out * out, axis=1, keepdims=True) + 1e-06)
-        gain = gain_ref[:, j * W : j * W + W]
-        n_buf[tp, :, j * W : j * W + W] = (out * scale * gain).astype(BF16)
-
-    chip = tp // 2
-    partner = chip * 2 + 1 - core
-
-    def n_copy(d):
-        other = lax.rem(chip + d, 4) * 2 + core
+        entering = right3(split2(state[...]))
+        gain = jnp.where(
+            lax.rem(y, 2) == 0, gain_ref[:, :W], gain_ref[:, W:]
+        )
+        for dy in (2, 1, 3, 0):
+            s = lax.rem(y + dy, n_y)
+            out = mm(pre_m[s], entering) + pre_n[s]
+            scale = lax.rsqrt(jnp.mean(out * out, axis=1, keepdims=True) + 1e-06)
+            done = (out * scale * gain).astype(BF16)
+            n_send[s] = done
+            if dy == 0:
+                n_buf[chip * 4 + y] = done
+            for dx in (2, 1, 3, 0):
+                if dx or dy:
+                    n_copy(dy, dx).start()
+
+    def pass_on(j, dx):
+        head = lax.rem(chip + dx, 4) * 4 + 2 * core + j
         return pltpu.make_async_remote_copy(
-            n_buf.at[tp], n_buf.at[tp], n_ssem.at[d], n_rsem.at[tp], (ctx, other), MESH
-        )
-
-    def pass_on(d):
-        src = lax.rem(chip + d, 4) * 2 + core
-        return pltpu.make_async_remote_copy(
-            n_buf.at[src], n_buf.at[src], f_ssem.at[d], n_rsem.at[src], (ctx, partner), MESH
-        )
-
-    def arrived(src):
+            n_buf.at[head], n_buf.at[head], f_ssem.at[j * 4 + dx], n_rsem.at[head],
+            (ctx, partner), MESH,
+        )
+
+    def arrived(head):
         pltpu.make_async_remote_copy(
-            n_buf.at[src], n_buf.at[src], f_ssem.at[0], n_rsem.at[src], (ctx, partner), MESH
+            n_buf.at[head], n_buf.at[head], f_ssem.at[0], n_rsem.at[head], (ctx, partner), MESH
         ).wait_recv()
 
     def w_arrived(src):
@@ -521,49 +557,67 @@
             w_buf.at[src], w_buf.at[src], w_ssem.at[0], w_rsem.at[src], (ctx, partner), MESH
         ).wait_recv()
 
-    for d in (2, 1, 3):
-        n_copy(d).start()
-    pass_on(0).start()
-    w_own.wait()
-    total = mm(n_buf[tp], w_buf[tp])
-    w_arrived(partner)
-    arrived(partner)
-    total = total + mm(n_buf[partner], w_buf[partner])
-    for d in (1, 3, 2):
-        src = lax.rem(chip + d, 4) * 2 + core
-        arrived(src)
-        pass_on(d).start()
+    def term(first, src):
+        both = jnp.concatenate([n_buf[first], n_buf[first + 1]], axis=1)
+        return mm(both, w_buf[src])
+
+    total = None
+    for dx in (0, 1, 3, 2):
+        src = lax.rem(chip + dx, 4) * 2 + core
+        first = lax.rem(chip + dx, 4) * 4 + 2 * core
+        for j in range(2):
+            if dx == 0:
+
+                @pl.when(y != 2 * core + j)
+                def _():
+                    arrived(first + j)
+
+            else:
+                arrived(first + j)
+            pass_on(j, dx).start()
+        if dx == 0:
+            w_own.wait()
+        else:
+            w_arrived(src)
+        part = term(first, src)
+        total = part if total is None else total + part
+    for dx in (0, 1, 3, 2):
+        src = lax.rem(chip + dx, 4) * 2 + 1 - core
+        first = lax.rem(chip + dx, 4) * 4 + 2 * (1 - core)
         w_arrived(src)
-        total = total + mm(n_buf[src], w_buf[src])
-    for d in (1, 3, 2):
-        src = lax.rem(chip + d, 4) * 2 + 1 - core
-        w_arrived(src)
-        arrived(src)
-        total = total + mm(n_buf[src], w_buf[src])
+        arrived(first)
+        arrived(first + 1)
+        total = total + term(first, src)
     o_ref[...] = total.astype(BF16)
 
     for copy in w_copies:
         copy.wait_send()
-    for d in range(4):
-        pass_on(d).wait_send()
-    for d in range(1, 4):
-        n_copy(d).wait_send()
     for j in range(2):
+        for dx in range(4):
+            pass_on(j, dx).wait_send()
 
         @pl.when(y != 2 * core + j)
         def _():
             y_copy(j).wait_send()
+            r_copy(j).wait_send()
 
     @pl.when(y // 2 == core)
     def _():
         for d in range(1, 4):
             l_copy(d).wait_send()
 
-            @pl.when(zg + d < 4)
+            @pl.when(zg == 0)
+            def _():
+                h_copy_first(d).wait_send()
+
+            @pl.when((zg > 0) & (zg + d < 4))
             def _():
                 h_copy(d).wait_send()
 
-            s_copy(lax.rem(y + d, n_y), mine).wait_send()
+        for dy in range(n_y):
+            for dx in range(4):
+                if dx or dy:
+                    n_copy(dy, dx).wait_send()
 
 
 def local(queries, key_vectors, value_vectors, strengths, log_gate, out_gain, out_weight):
@@ -589,14 +643,13 @@
             pltpu.VMEM((4, 2, W, W), BF16),
             pltpu.VMEM((2, W, W), BF16),
             pltpu.VMEM((4, 2, W, W), BF16),
-            pltpu.VMEM((n_y, W, 2 * W), BF16),
+            pltpu.VMEM((n_y, W, 3 * W), BF16),
             pltpu.VMEM((n_y, W, W), F32),
             pltpu.VMEM((W, W), F32),
+            pltpu.VMEM((2, 2, W, W), BF16),
+            pltpu.VMEM((n_y, 2, W, W), BF16),
             pltpu.VMEM((n_y, W, W), BF16),
-            pltpu.VMEM((2, W, W), BF16),
-            pltpu.VMEM((2, W, 2 * W), BF16),
-            pltpu.VMEM((2, W, W), F32),
-            pltpu.VMEM((n_tp, W, 2 * W), BF16),
+            pltpu.VMEM((2 * n_tp, W, W), BF16),
             dma((n_tp,)),
             dma((n_tp,)),
             dma,
@@ -606,11 +659,11 @@
             dma((4,)),
             dma((4,)),
             dma((4,)),
+            dma((2,)),
             dma((n_y,)),
-            dma((2,)),
-            dma((4,)),
-            dma((n_tp,)),
-            dma((4,)),
+            dma((16,)),
+            dma((16,)),
+            dma((8,)),
             dma((4,)),
             pltpu.SemaphoreType.REGULAR,
         ],

time: 45.7 us -> 43 us (0.941); the launches traced: 45.5 us -> 42.2 us
  Pallas kernels: 43.9 us -> 40.6 us
    pallas_call x1, Pallas kernels: 43.9 us -> 40.6 us  [local(): pl.pallas_call(functools.partial(kernel, n_y, n_tp), out_shape=jax.ShapeD...]
where the time goes in v3:
time: 43 us; the launch traced here: 42.2 us
  Pallas kernels  40.6 us (94%)
  local copies, waits for them, and re-layouts  1.57 us (4%)
    pallas_call x1, Pallas kernels, local(): pl.pallas_call(functools.partial(kernel, n_y, n_tp), out_shape=jax.ShapeD...  40.6 us
    unnamed x1, local copies, waits for them, and re-layouts  1.57 us

profile of v3, /device:TPU:1, one launch (start us, length us, event | category | flops | bytes accessed | tf_op | source)
XLA Modules:
  0.0 42.2 jit_solution(1674023148081678608)
XLA Ops:
  0.0 40.6 %shard_map.73 = bf16[128,512]{1,0:T(8,128)(2,1)} custom-call(bf16[128,256]{1,0:T(8,128)(2,1)} %q_ref.1, bf16[128,2,256]{2,1,0:T(2,128)(2,1)} %k_ref.1, bf16[128,2,256]{2,1,0:T(2,128)(2,1)} %v_ref.1, f32[4,128]{1,0:T(4,128)} %bitcast.2, f32[2,128]{1,0:T(2,128)} %gate_ref.1, f32[1,256]{1,0:T(1,128)} %bitcast.3, bf16[256,4096]{1,0:T(8,128)(2,1)} %w_ref.1), custom_call_target="tpu_custom_call" | custom-call | tf_op jit(solution)/shard_map/pallas_call | solution.py:631
  40.6 1.6 %copy.9 = bf16[128,512]{1,0:T(8,128)(2,1)} copy(bf16[128,512]{1,0:T(8,128)(2,1)} %shard_map.73) | data formatting | bytes 262144

commit v4 on v3

--- a/solution.py
+++ b/solution.py
@@ -185,8 +185,8 @@
     return out
 
 
-def local_reads(query, key, made):
-    _, _, write, c_row, inv_row, g3 = made
+def local_reads(query, key, gate, write, c_row, inv_rows):
+    g3 = jnp.concatenate(split3(jnp.broadcast_to(gate, (W, W))), axis=1)
     row = iota((W, W), 0)
     col = iota((W, W), 1)
     upto = bits(col <= row)
@@ -197,30 +197,48 @@
         cols = slice(a * W, a * W + W)
         diff = minus_rows(c_tok, c_row[:, cols])
         ratio = jnp.exp(jnp.where(col + a * W <= 2 * row + 1, diff, -1e30))
-        weights.append(ratio * times_rows(seen[:, cols], inv_row[a]))
-    both = x3(jnp.concatenate(weights, axis=1), write)
+        weights.append(ratio * times_rows(seen[:, cols], inv_rows[:, cols]))
+    both = dot_pairs(split2(jnp.concatenate(weights, axis=1)), write)
     return jnp.exp(c_tok) * query.astype(F32) - both[:, :W], both[:, W:]
 
 
+def apply(left, right):
+    if left[1] is None and right[1] is None:
+        return mm(left[0], right[0])
+    if left[1] is None:
+        return mm(
+            jnp.concatenate([left[0], left[0]], axis=1), jnp.concatenate(right, axis=0)
+        )
+    if right[1] is None:
+        return dot_pair_one(left, right[0])
+    return dot_pairs(left, right)
+
+
 def compose(later, earlier):
-    move = dot_pairs(later[0], earlier[0])
-    offset = dot_pairs(later[0], split2(earlier[1])) + later[1]
+    move = apply(later[0], earlier[0])
+    offset = apply(later[0], split2(earlier[1])) + later[1]
     return split2(move), offset
 
 
 def kernel(
     n_y,
     n_tp,
-    q_ref,
-    k_ref,
-    v_ref,
-    beta_ref,
-    gate_ref,
-    gain_ref,
+    q_hbm,
+    k_hbm,
+    v_hbm,
+    beta_hbm,
+    gate_hbm,
+    gain_hbm,
     w_ref,
     o_ref,
     k_buf,
     v_buf,
+    q_ref,
+    beta_ref,
+    gate_ref,
+    gain_ref,
+    written,
+    rows_buf,
     w_buf,
     y_send,
     y_recv,
@@ -265,13 +283,20 @@
         return zz * n_y + yy
 
     loads = []
-    for i, (ref, buf) in enumerate(((k_ref, k_buf), (v_ref, v_buf))):
+    for i, (ref, buf) in enumerate(((k_hbm, k_buf), (v_hbm, v_buf))):
         for h in range(2):
             copy = pltpu.make_async_copy(
                 ref.reshape(2 * W, 2 * W).at[:, pl.ds(h * W, W)], buf.at[h], i_sem.at[2 * i + h]
             )
             copy.start()
             loads.append(copy)
+
+    for i, (ref, buf) in enumerate(
+        ((beta_hbm, beta_ref), (gate_hbm, gate_ref), (q_hbm, q_ref), (gain_hbm, gain_ref))
+    ):
+        copy = pltpu.make_async_copy(ref, buf, i_sem.at[4 + i])
+        copy.start()
+        loads.append(copy)
 
     barrier = pltpu.get_barrier_semaphore()
     near = [(ctx, lax.rem(tp + d, n_tp)) for d in range(1, n_tp)]
@@ -298,6 +323,40 @@
     beta1 = [beta_ref[2 + h : 3 + h, :] for h in range(2)]
     gates = [gate_ref[h : h + 1, :] for h in range(2)]
 
+    def y_copy(j):
+        owner = 2 * core + j
+        return pltpu.make_async_remote_copy(
+            y_send.at[j], y_recv.at[y], y_ssem.at[j], y_rsem.at[y], (at(z, owner), tp), MESH
+        )
+
+    def r_copy(j):
+        owner = 2 * core + j
+        return pltpu.make_async_remote_copy(
+            r_send.at[j], r_recv.at[y], r_ssem.at[j], r_rsem.at[y], (at(z, owner), tp), MESH
+        )
+
+    @pl.when(tp >= 0)
+    def _():
+        made = local_maps(masks, keys, values, beta0, beta1, gates)
+        for j in range(2):
+            move = made[j][0].astype(BF16)
+            offset = made[j][1].astype(BF16)
+            hi, lo = split2(made[j][2])
+            written[j, 0] = hi
+            written[j, 1] = lo
+            rows_buf[j, 0] = made[j][3]
+            rows_buf[j, 1] = jnp.concatenate(made[j][4], axis=1)
+
+            @pl.when(y == 2 * core + j)
+            def _():
+                y_recv[y, 0] = move
+                y_recv[y, 1] = offset
+
+            @pl.when(y != 2 * core + j)
+            def _():
+                y_send[j, 0] = move
+                y_send[j, 1] = offset
+
     pl.semaphore_wait(barrier, len(near) + zg)
     for d in range(1, 4):
 
@@ -308,6 +367,12 @@
                 device_id_type=MESH,
             )
 
+    for j in range(2):
+
+        @pl.when(y != 2 * core + j)
+        def _():
+            y_copy(j).start()
+
     def w_columns(owner):
         return w_ref.at[:, pl.ds(pl.multiple_of(owner * wide, wide), wide)]
 
@@ -323,40 +388,13 @@
     w_own = pltpu.make_async_copy(w_columns(tp), w_buf.at[tp], w_lsem)
     w_own.start()
 
-    def y_copy(j):
-        owner = 2 * core + j
-        return pltpu.make_async_remote_copy(
-            y_send.at[j], y_recv.at[y], y_ssem.at[j], y_rsem.at[y], (at(z, owner), tp), MESH
-        )
-
-    def r_copy(j):
-        owner = 2 * core + j
-        return pltpu.make_async_remote_copy(
-            r_send.at[j], r_recv.at[y], r_ssem.at[j], r_rsem.at[y], (at(z, owner), tp), MESH
-        )
-
     @pl.when(tp >= 0)
     def _():
-        made = local_maps(masks, keys, values, beta0, beta1, gates)
         for j in range(2):
-            move = split2(made[j][0])
-            offset = made[j][1].astype(BF16)
-
-            @pl.when(y == 2 * core + j)
-            def _():
-                y_recv[y, 0] = move[0]
-                y_recv[y, 1] = move[1]
-                y_recv[y, 2] = offset
-
-            @pl.when(y != 2 * core + j)
-            def _():
-                y_send[j, 0] = move[0]
-                y_send[j, 1] = move[1]
-                y_send[j, 2] = offset
-                y_copy(j).start()
-
-        for j in range(2):
-            eff, loc = local_reads(q_ref[:, j * W : j * W + W], keys[j], made[j])
+            eff, loc = local_reads(
+                q_ref[:, j * W : j * W + W], k_buf[j], gate_ref[j : j + 1, :],
+                (written[j, 0], written[j, 1]), rows_buf[j, 0], rows_buf[j, 1],
+            )
             eff = eff.astype(BF16)
             loc = loc.astype(BF16)
 
@@ -421,7 +459,7 @@
                 ).wait_recv()
 
         part = [
-            ((y_recv[s, 0], y_recv[s, 1]), y_recv[s, 2].astype(F32)) for s in range(n_y)
+            ((y_recv[s, 0], None), y_recv[s, 1].astype(F32)) for s in range(n_y)
         ]
         first_two = compose(part[1], part[0])
         last_two = compose(part[3], part[2])
@@ -438,8 +476,7 @@
                 l_recv.at[src], l_recv.at[src], l_ssem.at[d], l_rsem.at[src],
                 (at(zg * 4 + src, y), tp), MESH,
             ).wait_recv()
-        none = jnp.zeros((W, W), BF16)
-        grp = [((l_recv[s, 0], none), l_recv[s, 1].astype(F32)) for s in range(4)]
+        grp = [((l_recv[s, 0], None), l_recv[s, 1].astype(F32)) for s in range(4)]
         low_two = compose(grp[1], grp[0])
         high_two = compose(grp[3], grp[2])
         total = compose(high_two, low_two)
@@ -631,14 +668,20 @@
     return pl.pallas_call(
         functools.partial(kernel, n_y, n_tp),
         out_shape=jax.ShapeDtypeStruct((tokens, width), BF16),
-        in_specs=[vmem, hbm, hbm, vmem, vmem, vmem, hbm],
+        in_specs=[hbm] * 7,
         out_specs=vmem,
         scratch_shapes=[
             pltpu.VMEM((2, 2 * W, W), BF16),
             pltpu.VMEM((2, 2 * W, W), BF16),
+            pltpu.VMEM((W, 2 * W), BF16),
+            pltpu.VMEM((4, W), F32),
+            pltpu.VMEM((2, W), F32),
+            pltpu.VMEM((1, 2 * W), F32),
+            pltpu.VMEM((2, 2, 2 * W, 2 * W), BF16),
+            pltpu.VMEM((2, 2, 8, 2 * W), F32),
             pltpu.VMEM((n_tp, 2 * W, width), BF16),
-            pltpu.VMEM((2, 3, W, W), BF16),
-            pltpu.VMEM((n_y, 3, W, W), BF16),
+            pltpu.VMEM((2, 2, W, W), BF16),
+            pltpu.VMEM((n_y, 2, W, W), BF16),
             pltpu.VMEM((2, W, W), BF16),
             pltpu.VMEM((4, 2, W, W), BF16),
             pltpu.VMEM((2, W, W), BF16),
@@ -664,7 +707,7 @@
             dma((16,)),
             dma((16,)),
             dma((8,)),
-            dma((4,)),
+            dma((8,)),
             pltpu.SemaphoreType.REGULAR,
         ],
         compiler_params=pltpu.CompilerParams(collective_id=0, has_side_effects=True),

time: 43 us -> 41.6 us (0.967); the launches traced: 42.2 us -> 41.4 us
  Pallas kernels: 40.6 us -> 39.9 us
    pallas_call x1, Pallas kernels: 40.6 us -> 39.9 us  [local(): pl.pallas_call(functools.partial(kernel, n_y, n_tp), out_shape=jax.ShapeD...]
where the time goes in v4:
time: 41.6 us; the launch traced here: 41.4 us
  Pallas kernels  39.9 us (96%)
  local copies, waits for them, and re-layouts  1.57 us (4%)
    pallas_call x1, Pallas kernels, local(): pl.pallas_call(functools.partial(kernel, n_y, n_tp), out_shape=jax.ShapeD...  39.9 us
    unnamed x1, local copies, waits for them, and re-layouts  1.57 us

profile of v4, /device:TPU:1, one launch (start us, length us, event | category | flops | bytes accessed | tf_op | source)
XLA Modules:
  0.0 41.4 jit_solution(3598003842292481764)
XLA Ops:
  0.0 39.9 %shard_map.73 = bf16[128,512]{1,0:T(8,128)(2,1)} custom-call(bf16[128,256]{1,0:T(8,128)(2,1)} %q_hbm.1, bf16[128,2,256]{2,1,0:T(2,128)(2,1)} %k_hbm.1, bf16[128,2,256]{2,1,0:T(2,128)(2,1)} %v_hbm.1, f32[4,128]{1,0:T(4,128)} %bitcast.2, f32[2,128]{1,0:T(2,128)} %gate_hbm.1, f32[1,256]{1,0:T(1,128)} %bitcast.3, bf16[256,4096]{1,0:T(8,128)(2,1)} %w_ref.1), custom_call_target="tpu_custom_call" | custom-call | tf_op jit(solution)/shard_map/pallas_call | solution.py:668
  39.9 1.6 %copy.9 = bf16[128,512]{1,0:T(8,128)(2,1)} copy(bf16[128,512]{1,0:T(8,128)(2,1)} %shard_map.73) | data formatting | bytes 262144

commit v5 on v4

--- a/solution.py
+++ b/solution.py
@@ -268,6 +268,8 @@
     n_rsem,
     f_ssem,
     i_sem,
+    u_ssem,
+    u_rsem,
     ready,
 ):
     ctx = lax.axis_index("ctx")
@@ -376,17 +378,50 @@
     def w_columns(owner):
         return w_ref.at[:, pl.ds(pl.multiple_of(owner * wide, wide), wide)]
 
-    w_copies = []
-    for d, flip in ((2, 0), (2, 1), (1, 0), (3, 0), (1, 1), (3, 1), (0, 1)):
-        owner = lax.rem(tp // 2 + d, 4) * 2 + lax.rem(core + flip, 2)
-        d = 2 * d + flip
-        copy = pltpu.make_async_remote_copy(
-            w_columns(owner), w_buf.at[tp], w_ssem.at[d], w_rsem.at[tp], (ctx, owner), MESH
-        )
-        copy.start()
-        w_copies.append(copy)
+    side = lax.rem(y, 2)
+    chip = tp // 2
+    partner = chip * 2 + 1 - core
+
+    def w_copy(d, flip):
+        owner = lax.rem(chip + d, 4) * 2 + lax.rem(core + flip, 2)
+        return pltpu.make_async_remote_copy(
+            w_columns(owner), w_buf.at[tp], w_ssem.at[2 * d + flip], w_rsem.at[tp],
+            (ctx, owner), MESH,
+        )
+
+    w_far = ((1, 0), (3, 0), (1, 1), (3, 1), (2, 0), (2, 1))
+
+    @pl.when(core == side)
+    def _():
+        for d, flip in w_far:
+            w_copy(d, flip).start()
+
+    w_copy(0, 1).start()
     w_own = pltpu.make_async_copy(w_columns(tp), w_buf.at[tp], w_lsem)
     w_own.start()
+
+    def w_half(d, k):
+        x = lax.rem(chip + d, 4)
+        half = w_buf.at[x * 2 + side, pl.ds(k * W, W)]
+        return pltpu.make_async_remote_copy(
+            half, half, u_ssem.at[2 * d + k], u_rsem.at[2 * x + k],
+            (at(z, lax.rem(y + (1 if k == 0 else n_y - 1), n_y)), tp), MESH,
+        )
+
+    def w_share(d):
+        src = lax.rem(chip + d, 4) * 2 + side
+        pltpu.make_async_remote_copy(
+            w_buf.at[src], w_buf.at[src], w_ssem.at[0], w_rsem.at[src], (ctx, partner), MESH
+        ).wait_recv()
+        for k in range(2):
+            w_half(d, k).start()
+
+    def w_shared(d, k):
+        x = lax.rem(chip + d, 4)
+        half = w_buf.at[x * 2 + 1 - side, pl.ds(k * W, W)]
+        pltpu.make_async_remote_copy(
+            half, half, u_ssem.at[0], u_rsem.at[2 * x + k], (ctx, partner), MESH
+        ).wait_recv()
 
     @pl.when(tp >= 0)
     def _():
@@ -427,9 +462,6 @@
             (at(lax.rem(z + 4 * d, 16), y), tp), MESH,
         )
 
-    chip = tp // 2
-    partner = chip * 2 + 1 - core
-
     def n_copy(dy, dx):
         s = lax.rem(y + dy, n_y)
         other = lax.rem(chip + dx, 4) * 2 + core
@@ -445,6 +477,8 @@
 
     @pl.when(y // 2 != core)
     def _():
+        for d in (1, 3, 2):
+            w_share(d)
         ready_wait()
 
     @pl.when(y // 2 == core)
@@ -494,6 +528,9 @@
             def _():
                 h_copy(d).start()
 
+        w_share(1)
+        w_share(3)
+
         @pl.when(tp >= 0)
         def _():
             row = iota((W, W), 0)
@@ -540,6 +577,7 @@
                 ) + r_recv[s, 1].astype(F32)
             state[...] = jnp.zeros((W, W), F32)
 
+        w_share(2)
         for s in range(3):
 
             @pl.when(s < zg)
@@ -589,10 +627,11 @@
             n_buf.at[head], n_buf.at[head], f_ssem.at[0], n_rsem.at[head], (ctx, partner), MESH
         ).wait_recv()
 
-    def w_arrived(src):
-        pltpu.make_async_remote_copy(
-            w_buf.at[src], w_buf.at[src], w_ssem.at[0], w_rsem.at[src], (ctx, partner), MESH
-        ).wait_recv()
+    def w_ready(dx, of):
+        @pl.when(of != side)
+        def _():
+            for k in range(2):
+                w_shared(dx, k)
 
     def term(first, src):
         both = jnp.concatenate([n_buf[first], n_buf[first + 1]], axis=1)
@@ -615,20 +654,35 @@
         if dx == 0:
             w_own.wait()
         else:
-            w_arrived(src)
+            w_ready(dx, core)
         part = term(first, src)
         total = part if total is None else total + part
     for dx in (0, 1, 3, 2):
         src = lax.rem(chip + dx, 4) * 2 + 1 - core
         first = lax.rem(chip + dx, 4) * 4 + 2 * (1 - core)
-        w_arrived(src)
+        if dx == 0:
+            pltpu.make_async_remote_copy(
+                w_buf.at[partner], w_buf.at[partner], w_ssem.at[0], w_rsem.at[partner],
+                (ctx, partner), MESH,
+            ).wait_recv()
+        else:
+            w_ready(dx, 1 - core)
         arrived(first)
         arrived(first + 1)
         total = total + term(first, src)
     o_ref[...] = total.astype(BF16)
 
-    for copy in w_copies:
-        copy.wait_send()
+    w_copy(0, 1).wait_send()
+
+    @pl.when(core == side)
+    def _():
+        for d, flip in w_far:
+            w_copy(d, flip).wait_send()
+
+    for d in range(1, 4):
+        for k in range(2):
+            w_half(d, k).wait_send()
+
     for j in range(2):
         for dx in range(4):
             pass_on(j, dx).wait_send()
@@ -708,6 +762,8 @@
             dma((16,)),
             dma((8,)),
             dma((8,)),
+            dma((8,)),
+            dma((8,)),
             pltpu.SemaphoreType.REGULAR,
         ],
         compiler_params=pltpu.CompilerParams(collective_id=0, has_side_effects=True),

time: 41.6 us -> 40.1 us (0.964)
  the two profiles are of different devices: /device:TPU:1 before, /device:TPU:15 now
where the time goes in v5:
time: 40.1 us; the launch traced here: 39.9 us
  Pallas kernels  38.3 us (96%)
  local copies, waits for them, and re-layouts  1.57 us (4%)
    pallas_call x1, Pallas kernels, local(): pl.pallas_call(functools.partial(kernel, n_y, n_tp), out_shape=jax.ShapeD...  38.3 us
    unnamed x1, local copies, waits for them, and re-layouts  1.57 us

profile of v5, /device:TPU:15, one launch (start us, length us, event | category | flops | bytes accessed | tf_op | source)
XLA Modules:
  0.0 39.9 jit_solution(4073458605359968081)
XLA Ops:
  0.0 38.3 %shard_map.73 = bf16[128,512]{1,0:T(8,128)(2,1)} custom-call(bf16[128,256]{1,0:T(8,128)(2,1)} %q_hbm.1, bf16[128,2,256]{2,1,0:T(2,128)(2,1)} %k_hbm.1, bf16[128,2,256]{2,1,0:T(2,128)(2,1)} %v_hbm.1, f32[4,128]{1,0:T(4,128)} %bitcast.2, f32[2,128]{1,0:T(2,128)} %gate_hbm.1, f32[1,256]{1,0:T(1,128)} %bitcast.3, bf16[256,4096]{1,0:T(8,128)(2,1)} %w_ref.1), custom_call_target="tpu_custom_call" | custom-call | tf_op jit(solution)/shard_map/pallas_call | solution.py:722
  38.3 1.6 %copy.9 = bf16[128,512]{1,0:T(8,128)(2,1)} copy(bf16[128,512]{1,0:T(8,128)(2,1)} %shard_map.73) | data formatting | bytes 262144

commit v6 on v5

--- a/solution.py
+++ b/solution.py
@@ -384,44 +384,50 @@
 
     def w_copy(d, flip):
         owner = lax.rem(chip + d, 4) * 2 + lax.rem(core + flip, 2)
-        return pltpu.make_async_remote_copy(
-            w_columns(owner), w_buf.at[tp], w_ssem.at[2 * d + flip], w_rsem.at[tp],
+        rows = pl.ds(pl.multiple_of(side * W, W), W)
+        columns = pl.ds(pl.multiple_of(owner * wide, wide), wide)
+        return pltpu.make_async_remote_copy(
+            w_ref.at[rows, columns], w_buf.at[tp, rows], w_ssem.at[2 * d + flip], w_rsem.at[tp],
             (ctx, owner), MESH,
         )
 
     w_far = ((1, 0), (3, 0), (1, 1), (3, 1), (2, 0), (2, 1))
-
-    @pl.when(core == side)
-    def _():
-        for d, flip in w_far:
-            w_copy(d, flip).start()
-
-    w_copy(0, 1).start()
+    for d, flip in w_far:
+        w_copy(d, flip).start()
+    w_near = pltpu.make_async_remote_copy(
+        w_columns(partner), w_buf.at[tp], w_ssem.at[1], w_rsem.at[tp], (ctx, partner), MESH
+    )
+    w_near.start()
     w_own = pltpu.make_async_copy(w_columns(tp), w_buf.at[tp], w_lsem)
     w_own.start()
 
-    def w_half(d, k):
+    def w_quarter(d, c, k):
         x = lax.rem(chip + d, 4)
-        half = w_buf.at[x * 2 + side, pl.ds(k * W, W)]
-        return pltpu.make_async_remote_copy(
-            half, half, u_ssem.at[2 * d + k], u_rsem.at[2 * x + k],
+        part = w_buf.at[x * 2 + c, pl.ds(pl.multiple_of(side * W + k * (W // 2), W // 2), W // 2)]
+        return pltpu.make_async_remote_copy(
+            part, part, u_ssem.at[4 * d + 2 * c + k], u_rsem.at[4 * x + 2 * c + k],
             (at(z, lax.rem(y + (1 if k == 0 else n_y - 1), n_y)), tp), MESH,
         )
 
     def w_share(d):
-        src = lax.rem(chip + d, 4) * 2 + side
-        pltpu.make_async_remote_copy(
-            w_buf.at[src], w_buf.at[src], w_ssem.at[0], w_rsem.at[src], (ctx, partner), MESH
-        ).wait_recv()
+        for c in range(2):
+            src = lax.rem(chip + d, 4) * 2 + c
+            part = w_buf.at[src, pl.ds(pl.multiple_of(side * W, W), W)]
+            pltpu.make_async_remote_copy(
+                part, part, w_ssem.at[0], w_rsem.at[src], (ctx, partner), MESH
+            ).wait_recv()
+            for k in range(2):
+                w_quarter(d, c, k).start()
+
+    def w_ready(d, c):
+        x = lax.rem(chip + d, 4)
         for k in range(2):
-            w_half(d, k).start()
-
-    def w_shared(d, k):
-        x = lax.rem(chip + d, 4)
-        half = w_buf.at[x * 2 + 1 - side, pl.ds(k * W, W)]
-        pltpu.make_async_remote_copy(
-            half, half, u_ssem.at[0], u_rsem.at[2 * x + k], (ctx, partner), MESH
-        ).wait_recv()
+            part = w_buf.at[
+                x * 2 + c, pl.ds(pl.multiple_of((1 - side) * W + k * (W // 2), W // 2), W // 2)
+            ]
+            pltpu.make_async_remote_copy(
+                part, part, u_ssem.at[0], u_rsem.at[4 * x + 2 * c + k], (ctx, partner), MESH
+            ).wait_recv()
 
     @pl.when(tp >= 0)
     def _():
@@ -504,7 +510,10 @@
             l_copy(d).start()
         l_recv[zl, 0] = whole[0][0]
         l_recv[zl, 1] = whole[1].astype(BF16)
-        for d in range(1, 4):
+        for d in (1, 2, 3):
+            if d == 3:
+                w_share(1)
+                w_share(3)
             src = lax.rem(zl + d, 4)
             pltpu.make_async_remote_copy(
                 l_recv.at[src], l_recv.at[src], l_ssem.at[d], l_rsem.at[src],
@@ -527,9 +536,6 @@
             @pl.when((zg > 0) & (zg + d < 4))
             def _():
                 h_copy(d).start()
-
-        w_share(1)
-        w_share(3)
 
         @pl.when(tp >= 0)
         def _():
@@ -626,12 +632,6 @@
         pltpu.make_async_remote_copy(
             n_buf.at[head], n_buf.at[head], f_ssem.at[0], n_rsem.at[head], (ctx, partner), MESH
         ).wait_recv()
-
-    def w_ready(dx, of):
-        @pl.when(of != side)
-        def _():
-            for k in range(2):
-                w_shared(dx, k)
 
     def term(first, src):
         both = jnp.concatenate([n_buf[first], n_buf[first + 1]], axis=1)
@@ -672,16 +672,13 @@
         total = total + term(first, src)
     o_ref[...] = total.astype(BF16)
 
-    w_copy(0, 1).wait_send()
-
-    @pl.when(core == side)
-    def _():
-        for d, flip in w_far:
-            w_copy(d, flip).wait_send()
-
+    w_near.wait_send()
+    for d, flip in w_far:
+        w_copy(d, flip).wait_send()
     for d in range(1, 4):
-        for k in range(2):
-            w_half(d, k).wait_send()
+        for c in range(2):
+            for k in range(2):
+                w_quarter(d, c, k).wait_send()
 
     for j in range(2):
         for dx in range(4):
@@ -762,8 +759,8 @@
             dma((16,)),
             dma((8,)),
             dma((8,)),
-            dma((8,)),
-            dma((8,)),
+            dma((16,)),
+            dma((16,)),
             pltpu.SemaphoreType.REGULAR,
         ],
         compiler_params=pltpu.CompilerParams(collective_id=0, has_side_effects=True),

time: 40.1 us -> 39.5 us (0.985)
  the two profiles are of different devices: /device:TPU:15 before, /device:TPU:481 now
where the time goes in v6:
time: 39.5 us; the launch traced here: 39.3 us
  Pallas kernels  37.7 us (95%)
  local copies, waits for them, and re-layouts  1.57 us (4%)
    pallas_call x1, Pallas kernels, local(): pl.pallas_call(functools.partial(kernel, n_y, n_tp), out_shape=jax.ShapeD...  37.7 us
    unnamed x1, local copies, waits for them, and re-layouts  1.57 us

profile of v6, /device:TPU:481, one launch (start us, length us, event | category | flops | bytes accessed | tf_op | source)
XLA Modules:
  0.0 39.3 jit_solution(9963299640255659416)
XLA Ops:
  0.0 37.7 %shard_map.73 = bf16[128,512]{1,0:T(8,128)(2,1)} custom-call(bf16[128,256]{1,0:T(8,128)(2,1)} %q_hbm.1, bf16[128,2,256]{2,1,0:T(2,128)(2,1)} %k_hbm.1, bf16[128,2,256]{2,1,0:T(2,128)(2,1)} %v_hbm.1, f32[4,128]{1,0:T(4,128)} %bitcast.2, f32[2,128]{1,0:T(2,128)} %gate_hbm.1, f32[1,256]{1,0:T(1,128)} %bitcast.3, bf16[256,4096]{1,0:T(8,128)(2,1)} %w_ref.1), custom_call_target="tpu_custom_call" | custom-call | tf_op jit(solution)/shard_map/pallas_call | solution.py:719
  37.7 1.6 %copy.9 = bf16[128,512]{1,0:T(8,128)(2,1)} copy(bf16[128,512]{1,0:T(8,128)(2,1)} %shard_map.73) | data formatting | bytes 262144
